TPU v7x, 1024 devices: a whole 8x8x8 slice. The times are simulated.
1024 devices in a mesh: energy: 64 (over y, z), space: 16 (over x, core).
Axes of the slice: x: 8, y: 8, z: 8, core: 2. Of those that a mesh axis runs over, the one named last changes fastest.
Arguments:
- iso_green: bfloat16 [64, 32, 2, 192, 192], P('energy', 'space'), as said below
- coupling: bfloat16 [32, 192, 192], P('space')
- screened: bfloat16 [64, 32, 2, 192, 192], P('energy', 'space'), as said below
Outputs:
- sigma: bfloat16 [64, 32, 2, 192, 192], P('energy', 'space')
Inputs may be any that keep to these rules, and one draw needn't show every extreme that they name: `iso_green`: every complex [192, 192] block (real and imaginary parts) equals its own transpose. `screened`: every complex [192, 192] block (real and imaginary parts) equals its own transpose.
All inputs are finite; a program needn't handle non-finite values.
Results may differ from a plain program's by a relative error of at most 0.023.
Values may be sent and summed in bfloat16 or wider, within the bound.
No kernel may reach another device: no remote copies, remote signals or barrier semaphores. Data moves between devices by JAX's collectives and lax.ppermute only.
A program may use at most 32 MiB of HBM per device.

v0:
```python
import math

import jax
import jax.numpy as jnp
from jax import lax
from jax.sharding import PartitionSpec as P


def prefix_2(shard, axis, join, neutral):
    place = lax.axis_index(axis)
    gathered = jax.tree.map(
        lambda a, kind: lax.all_gather(a.astype(kind), axis),
        shard,
        jax.tree.map(lambda a: jnp.bfloat16 if a.dtype == jnp.float32 else a.dtype, shard),
    )
    state = jax.tree.map(lambda a, e: jnp.zeros_like(a) + jnp.asarray(e, a.dtype), shard, neutral)

    def one(turn, state):
        return join(
            state,
            jax.tree.map(
                lambda a, own: lax.dynamic_index_in_dim(a, turn, 0, False).astype(own.dtype),
                gathered,
                shard,
            ),
        )

    return lax.fori_loop(0, place, one, state)


def complex_product(operand, factor, pattern):
    left = jnp.concatenate([operand[:, 0], operand[:, 1]], axis=-1)
    fa_re = factor[:, 0]
    fa_im = factor[:, 1]
    if pattern == "ekl,eml->ekm":
        right_re = jnp.concatenate([fa_re, -fa_im], axis=-1)
        right_im = jnp.concatenate([fa_im, fa_re], axis=-1)
        right = jnp.stack([right_re, right_im], axis=1)
        return jnp.einsum("ekl,ecml->eckm", left, right, preferred_element_type=jnp.float32)
    right_re = jnp.concatenate([fa_re, -fa_im], axis=-2)
    right_im = jnp.concatenate([fa_im, fa_re], axis=-2)
    right = jnp.stack([right_re, right_im], axis=1)
    return jnp.einsum("ekl,eclm->eckm", left, right, preferred_element_type=jnp.float32)


def sandwich(carried, factor, source):
    middle = complex_product(carried, factor, "ekl,eml->ekm").astype(jnp.bfloat16)
    return (source.astype(jnp.float32) + complex_product(factor, middle, "ekl,elm->ekm")).astype(
        jnp.bfloat16
    )


def compose(earlier, latter):
    joined = complex_product(latter[0], earlier[0], "ekl,elm->ekm").astype(jnp.bfloat16)
    return (joined, sandwich(earlier[1], latter[0], latter[1]))


def fold_step(carried, inputs):
    return (compose(carried, inputs), None)


def apply_step(carried, inputs):
    updated = sandwich(carried, inputs[0], inputs[1])
    return (updated, updated)


def twiddle_tables(points):
    index_row = lax.iota(jnp.int32, points)
    phase_index = index_row[:, None] * index_row[None, :] % points
    angles = phase_index.astype(jnp.float32) * (2.0 * math.pi / points)
    return jnp.concatenate([jnp.cos(angles), jnp.sin(angles)], axis=0)


def convolve(operands):
    green_part, screen_part = operands
    points = green_part.shape[0]
    kept_shape = green_part.shape
    table = twiddle_tables(points)
    table_high = table.astype(jnp.bfloat16)
    table_rest = (table - table_high.astype(jnp.float32)).astype(jnp.bfloat16)
    green_flat = green_part.reshape(points, 2, -1)
    screen_flat = screen_part.reshape(points, 2, -1)
    width = green_flat.shape[2]
    joined = jnp.concatenate(
        [green_flat[:, 0], green_flat[:, 1], screen_flat[:, 0], screen_flat[:, 1]], axis=1
    )
    mixed = jnp.dot(table_high, joined, preferred_element_type=jnp.float32) + jnp.dot(
        table_rest, joined, preferred_element_type=jnp.float32
    )
    with_cos = mixed[:points]
    with_sin = mixed[points:]
    green_re = with_cos[:, :width] + with_sin[:, width : 2 * width]
    green_im = with_cos[:, width : 2 * width] - with_sin[:, :width]
    screen_re = with_cos[:, 2 * width : 3 * width] + with_sin[:, 3 * width :]
    screen_im = with_cos[:, 3 * width :] - with_sin[:, 2 * width : 3 * width]
    prod_re = green_re * screen_re - green_im * screen_im
    prod_im = green_re * screen_im + green_im * screen_re
    spectrum = jnp.concatenate([prod_re, prod_im], axis=1)
    back = jnp.dot(table, spectrum, precision=lax.Precision.HIGH)
    back_cos = back[:points]
    back_sin = back[points:]
    back_re = back_cos[:, :width] - back_sin[:, width:]
    back_im = back_cos[:, width:] + back_sin[:, :width]
    scaling = 1.0 / (points * math.sqrt(points))
    result = (
        jnp.concatenate([-back_im * scaling, back_re * scaling], axis=1)
        .reshape(kept_shape)
        .astype(jnp.bfloat16)
    )
    return lax.all_to_all(result, "energy", split_axis=0, concat_axis=2, tiled=True)


def shards(iso_green, coupling, screened):
    energies = iso_green.shape[0]
    blocks = iso_green.shape[1]
    order = iso_green.shape[3]
    groups = lax.axis_size("energy")
    green_blocks = jnp.moveaxis(iso_green, 1, 0)
    transfer_blocks = jnp.einsum(
        "ebckl,blm->beckm", iso_green, coupling, preferred_element_type=jnp.float32
    ).astype(jnp.bfloat16)
    initial_map = (transfer_blocks[0], green_blocks[0])
    aggregate = lax.scan(fold_step, initial_map, (transfer_blocks[1:], green_blocks[1:]))[0]
    unit_matrix = jnp.broadcast_to(jnp.eye(order, dtype=jnp.bfloat16), (energies, order, order))
    identity_map = (
        jnp.stack([unit_matrix, jnp.zeros_like(unit_matrix)], axis=1),
        jnp.zeros_like(aggregate[1]),
    )
    prefix = prefix_2(aggregate, "space", compose, identity_map)
    connected = lax.scan(apply_step, prefix[1], (transfer_blocks, green_blocks))[1]
    stacked_green = connected.transpose(1, 2, 0, 3, 4).reshape(energies, 2, blocks, order * order)
    stacked_screen = screened.transpose(0, 2, 1, 3, 4).reshape(energies, 2, blocks, order * order)
    green_sent = stacked_green.reshape(energies, 2, groups, -1)
    screen_sent = stacked_screen.reshape(energies, 2, groups, -1)
    returned = convolve(
        (
            lax.all_to_all(green_sent, "energy", split_axis=2, concat_axis=0, tiled=True),
            lax.all_to_all(screen_sent, "energy", split_axis=2, concat_axis=0, tiled=True),
        )
    )
    returned = returned.reshape(energies, 2, blocks, -1)
    return returned.reshape(energies, 2, blocks, order, order).transpose(0, 2, 1, 3, 4)


def solution(mesh):
    in_specs = (
        P("energy", "space", None, None, None),
        P("space", None, None),
        P("energy", "space", None, None, None),
    )
    out_specs = P("energy", "space", None, None, None)
    return jax.shard_map(shards, mesh=mesh, in_specs=in_specs, out_specs=out_specs, check_vma=False)
```

profile of v0, /device:TPU:14, one launch (start us, length us, event | category | flops | bytes accessed | tf_op | source)
XLA Modules:
  0.0 225.4 jit_solution(15456304736760513779)
XLA Ops:
  7.5 1.2 convolution_convert_fusion.2
  12.6 1.0 copy.65
  13.7 23.4 %all-to-all-start.1 = ((bf16[1,2,64,1152]{3,1,0,2:T(2,128)(2,1)}), bf16[1,2,64,1152]{3,1,0,2:T(2,128)(2,1)S(1)}, u32[]{:S(2)}, u32[]{:S(2)}) async-start(bf16[1,2,64,1152]{3,1,0,2:T(2,128)(2,1)} %copy.65), calls=%async_computation.1 | async-start | bytes 589824 | tf_op jit(solution)/shard_map/all_to_all | solution.py:138
  37.1 30.5 %all-gather.5.cloned.1.call-done = bf16[16,2,192,192]{3,2,1,0:T(8,128)(2,1)} async-done(((bf16[1,2,192,192]{3,2,1,0:T(8,128)(2,1)}), bf16[16,2,192,192]{3,2,1,0:T(8,128)(2,1)}) %all-gather.5.cloned.1.call-update) | async-done | bytes 2359312 | tf_op jit(solution)/shard_map/all_gather | solution.py:12
  67.6 47.9 %all-gather.7.cloned.1.call-done = bf16[16,2,192,192]{3,2,1,0:T(8,128)(2,1)} async-done(((bf16[1,2,192,192]{3,2,1,0:T(8,128)(2,1)}), bf16[16,2,192,192]{3,2,1,0:T(8,128)(2,1)}) %all-gather.7.cloned.1.call-update) | async-done | bytes 2359312 | tf_op jit(solution)/shard_map/all_gather | solution.py:12
  115.5 46.2 %while.8 = (s32[]{:T(128)}, bf16[1,2,192,192]{2,3,1,0:T(8,128)(2,1)S(1)}, s32[]{:T(128)}, bf16[16,1,2,192,192]{4,3,2,0,1:T(8,128)(2,1)}, bf16[16,1,2,192,192]{4,...) while((s32[]{:T(128)}, bf16[1,2,192,192]{2,3,1,0:T(8,128)(2,1)S(1)}, s32[]{:T(128)}, ...), condition=%wide.region_1.2_spmd, body=%wide.region_0.1_spmd.sunk | while | flops 115679232 | bytes 4718719 | solution.py:28
  115.5 0.9 dynamic-slice_bitcast_fusion.4
  117.4 0.9 constant_dynamic-slice_fusion.2
  118.8 0.9 dynamic-slice_bitcast_fusion.4
  120.7 0.9 constant_dynamic-slice_fusion.2
  122.1 0.9 dynamic-slice_bitcast_fusion.4
  124.0 0.9 constant_dynamic-slice_fusion.2
  127.3 0.9 constant_dynamic-slice_fusion.2
  128.7 0.9 dynamic-slice_bitcast_fusion.4
  130.6 0.9 constant_dynamic-slice_fusion.2
  132.0 0.9 dynamic-slice_bitcast_fusion.4
  133.9 0.9 constant_dynamic-slice_fusion.2
  135.3 0.9 dynamic-slice_bitcast_fusion.4
  137.2 0.9 constant_dynamic-slice_fusion.2
  138.7 0.9 dynamic-slice_bitcast_fusion.4
  140.5 0.9 constant_dynamic-slice_fusion.2
  143.8 0.9 constant_dynamic-slice_fusion.2
  147.1 0.9 constant_dynamic-slice_fusion.2
  150.4 0.9 constant_dynamic-slice_fusion.2
  153.7 0.9 constant_dynamic-slice_fusion.2
  157.0 0.9 constant_dynamic-slice_fusion.2
  160.3 0.9 constant_dynamic-slice_fusion.2
  161.7 2.6 %while.30 = (s32[]{:T(128)}, bf16[1,2,192,192]{2,3,1,0:T(8,128)(2,1)S(1)}, bf16[2,1,2,192,192]{3,4,2,1,0:T(8,128)(2,1)S(1)}, bf16[2,1,2,192,192]{3,4,2,1,0:T(8,1...) while((s32[]{:T(128)}, bf16[1,2,192,192]{2,3,1,0:T(8,128)(2,1)S(1)}, ...), condition=%wide.region_3.4_spmd, body=%wide.region_2.3_spmd.sunk | while | flops 115679232 | bytes 4472909 | solution.py:130
  164.9 1.0 copy.62
  165.9 13.5 %all-to-all-start = ((bf16[1,2,64,1152]{3,1,0,2:T(2,128)(2,1)}), bf16[1,2,64,1152]{3,1,0,2:T(2,128)(2,1)S(1)}, u32[]{:S(2)}, u32[]{:S(2)}) async-start(bf16[1,2,64,1152]{3,1,0,2:T(2,128)(2,1)} %copy.62), calls=%async_computation | async-start | bytes 589824 | tf_op jit(solution)/shard_map/all_to_all | solution.py:137
  179.6 13.6 %all-to-all-done = bf16[1,2,64,1152]{3,1,0,2:T(2,128)(2,1)S(1)} async-done(((bf16[1,2,64,1152]{3,1,0,2:T(2,128)(2,1)}), bf16[1,2,64,1152]{3,1,0,2:T(2,128)(2,1)S(1)}, u32[]{:S(2)}, u32[]{:S(2)}) %all-to-all-start) | async-done | bytes 294944 | tf_op jit(solution)/shard_map/all_to_all | solution.py:137
  195.1 22.3 %all_to_all.45 = bf16[64,2,1,1152]{3,1,2,0:T(2,128)(2,1)S(1)} all-to-all(bf16[64,2,1,1152]{3,1,2,0:T(2,128)(2,1)S(1)} %bitcast.306), channel_id=1, replica_groups=mesh['energy'=64,'space'=16] {'energy'}, dimensions={0} | all-to-all | bytes 589824 | tf_op jit(solution)/shard_map/all_to_all | solution.py:110
  (230 shorter events, 35.6 us)
Async XLA Ops:
  6.5 0.9 copy-start
  6.5 2.2 copy-start.1
  6.5 61.1 %all-gather.5.cloned.1.call-start = ((), (), s32[]{:S(2)}) async-start(), calls=%async_computation.3 | async-start | bytes 3342336 | tf_op jit(solution)/shard_map/all_gather | solution.py:12
  10.9 1.3 copy-start.2
  11.0 104.5 %all-gather.7.cloned.1.call-start = ((), (), s32[]{:S(2)}) async-start(), calls=%async_computation.4 | async-start | bytes 3342336 | tf_op jit(solution)/shard_map/all_gather | solution.py:12
  13.7 152.2 %all-to-all-start.1 = ((bf16[1,2,64,1152]{3,1,0,2:T(2,128)(2,1)}), bf16[1,2,64,1152]{3,1,0,2:T(2,128)(2,1)S(1)}, u32[]{:S(2)}, u32[]{:S(2)}) async-start(bf16[1,2,64,1152]{3,1,0,2:T(2,128)(2,1)} %copy.65), calls=%async_computation.1 | async-start | bytes 589824 | tf_op jit(solution)/shard_map/all_to_all | solution.py:138
  165.9 27.3 %all-to-all-start = ((bf16[1,2,64,1152]{3,1,0,2:T(2,128)(2,1)}), bf16[1,2,64,1152]{3,1,0,2:T(2,128)(2,1)S(1)}, u32[]{:S(2)}, u32[]{:S(2)}) async-start(bf16[1,2,64,1152]{3,1,0,2:T(2,128)(2,1)} %copy.62), calls=%async_computation | async-start | bytes 589824 | tf_op jit(solution)/shard_map/all_to_all | solution.py:137
Sparse Core Ops, SparseCore 0:
  11.1 56.5 all-gather.4
  70.3 45.1 all-gather.6
where the time goes:
time: 226 us; the launch traced here: 225 us
  waiting for transfers between devices  92 us (41%)
  local copies, waits for them, and re-layouts  38.4 us (17%)
  starting transfers between devices  36.9 us (16%)
  blocking collectives  22.3 us (10%)
  matrix products  15.2 us (7%)
  between operations  13.7 us (6%)
  other arithmetic  5.12 us (2%)
    all_gather x2, waiting for transfers between devices, prefix_2(): lax.all_gather(a.astype(kind), axis)  78.4 us
    all_to_all x1, starting transfers between devices, shards(): lax.all_to_all(screen_sent, 'energy', split_axis=2, concat_axis=0, tiled=...  23.4 us
    all_to_all x1, blocking collectives, convolve(): lax.all_to_all(result, 'energy', split_axis=0, concat_axis=2, tiled=True)  22.3 us
    dynamic_slice x28, local copies, waits for them, and re-layouts, one(): lax.dynamic_index_in_dim(a, turn, 0, False).astype(own.dtype)  15.1 us
    all_to_all x1, waiting for transfers between devices, shards(): lax.all_to_all(green_sent, 'energy', split_axis=2, concat_axis=0, tiled=T...  13.6 us
    all_to_all x1, starting transfers between devices, shards(): lax.all_to_all(green_sent, 'energy', split_axis=2, concat_axis=0, tiled=T...  13.5 us
    squeeze x14, local copies, waits for them, and re-layouts, one(): lax.dynamic_index_in_dim(a, turn, 0, False).astype(own.dtype)  13.2 us
    dot_general x18, matrix products, complex_product(): jnp.einsum('ekl,eclm->eckm', left, right, preferred_element_type=jnp.floa...  6.46 us
  transfers between devices with their start and end apart: 4, of which 3 were waited for; matrix products, arithmetic and copies ran while one was open for 23% of the time, Pallas kernels for 0%

commit v1 on v0

v1 whole, which is shorter than its diff:
```python
import math

import jax
import jax.numpy as jnp
import numpy as np
from jax import lax
from jax.experimental import pallas as pl
from jax.experimental.pallas import tpu as pltpu
from jax.sharding import PartitionSpec as P

F32 = jnp.float32
BF16 = jnp.bfloat16
TILE = 64

VM = pl.BlockSpec(memory_space=pltpu.VMEM)
SM = pl.BlockSpec(memory_space=pltpu.SMEM)


def dot_nn(a, b):
    return lax.dot_general(a, b, (((1,), (0,)), ((), ())), preferred_element_type=F32)


def dot_nt(a, b):
    return lax.dot_general(a, b, (((1,), (1,)), ((), ())), preferred_element_type=F32)


def complex_product(a, b, dot):
    a_re, a_im = a
    b_re, b_im = b
    return dot(a_re, b_re) - dot(a_im, b_im), dot(a_re, b_im) + dot(a_im, b_re)


def rounded(pair):
    return pair[0].astype(BF16), pair[1].astype(BF16)


def sandwich(carried, factor, source):
    middle = rounded(complex_product(carried, factor, dot_nt))
    re, im = complex_product(factor, middle, dot_nn)
    return rounded((source[0].astype(F32) + re, source[1].astype(F32) + im))


def pack(m):
    t = TILE
    return jnp.concatenate([m[:t, :], m[t : 2 * t, t:], m[2 * t :, 2 * t :]], axis=1)


def unpack(p):
    t = TILE
    p = p.astype(F32)
    t01, t02 = p[:, t : 2 * t], p[:, 2 * t : 3 * t]
    t11, t12 = p[:, 3 * t : 4 * t], p[:, 4 * t : 5 * t]
    top = p[:, : 3 * t]
    mid = jnp.concatenate([t01.T, t11, t12], axis=1)
    low = jnp.concatenate([t02.T, t12.T, p[:, 5 * t :]], axis=1)
    return jnp.concatenate([top, mid, low], axis=0).astype(BF16)


def load(ref, *at):
    return ref[(*at, 0)], ref[(*at, 1)]


def store(ref, pair, *at):
    ref[(*at, 0)] = pair[0]
    ref[(*at, 1)] = pair[1]


def local_kernel(green, coupling, screened, transfer, aggregate, packed):
    maps = []
    for b in range(2):
        k = coupling[b]
        g = load(green, b)
        t = rounded((dot_nn(g[0], k), dot_nn(g[1], k)))
        store(transfer, t, b)
        maps.append((t, g))
    (t0, g0), (t1, g1) = maps
    store(aggregate, rounded(complex_product(t1, t0, dot_nn)), 0)
    store(aggregate, sandwich(g0, t1, g1), 1)
    for b in range(2):
        for part in range(2):
            packed[2 * b + part] = pack(screened[b, part])


def compose_kernel(pairs, out):
    low = load(pairs, 0, 0), load(pairs, 0, 1)
    high = load(pairs, 1, 0), load(pairs, 1, 1)
    store(out, rounded(complex_product(high[0], low[0], dot_nn)), 0)
    store(out, sandwich(low[1], high[0], high[1]), 1)


def pair_kernel(pairs, out, end):
    low = load(pairs, 0, 0), load(pairs, 0, 1)
    high = load(pairs, 1, 0), load(pairs, 1, 1)
    store(out, rounded(complex_product(high[0], low[0], dot_nn)), 0)
    c = sandwich(low[1], high[0], high[1])
    store(out, c, 1)
    end[0] = pack(c[0])
    end[1] = pack(c[1])


def hop_kernel(hop, place, received, pair_map, end_in, prefix_in, end, prefix):
    mine = place[0] == hop

    @pl.when(mine)
    def _():
        before = unpack(received[0, 0]), unpack(received[0, 1])
        c = sandwich(before, load(pair_map, 0), load(pair_map, 1))
        end[0] = pack(c[0])
        end[1] = pack(c[1])
        prefix[...] = received[0]

    @pl.when(jnp.logical_not(mine))
    def _():
        end[...] = end_in[...]
        prefix[...] = prefix_in[...]


def final_kernel(hop, place, received, prefix_in, chips, cores, transfer, green, packed, state):
    mine = place[0] == hop

    @pl.when(mine)
    def _():
        state[0] = unpack(received[0, 0])
        state[1] = unpack(received[0, 1])

    @pl.when(jnp.logical_not(mine))
    def _():
        state[0] = unpack(prefix_in[0])
        state[1] = unpack(prefix_in[1])

    @pl.when(place[1] == 1)
    def _():
        store(state, sandwich(load(state), load(chips, 0, 0), load(chips, 0, 1)))

    @pl.when(place[2] == 1)
    def _():
        store(state, sandwich(load(state), load(cores, 0, 0), load(cores, 0, 1)))

    carried = load(state)
    for b in range(2):
        carried = sandwich(carried, load(transfer, b), load(green, b))
        packed[2 * b] = pack(carried[0])
        packed[2 * b + 1] = pack(carried[1])


def split(table):
    high = table.astype(jnp.bfloat16)
    return high, (table - high.astype(np.float32)).astype(jnp.bfloat16)


def tables(points):
    row = np.arange(points)
    angles = (row[:, None] * row[None, :] % points) * (2.0 * math.pi / points)
    cos, sin = np.cos(angles), np.sin(angles)
    forward = np.block([[cos, sin], [-sin, cos]]).astype(np.float32)
    scaling = 1.0 / (points * math.sqrt(points))
    inverse = (np.block([[-sin, -cos], [cos, -sin]]) * scaling).astype(np.float32)
    return np.concatenate(split(forward), axis=1), np.concatenate(split(inverse), axis=1)


def convolve_kernel(forward, inverse, values, out):
    half = values.shape[1] // 2
    width = half // 4
    x = values[...]
    re = jnp.concatenate([x[:, s : s + width] for s in range(0, 2 * half, 2 * width)], axis=1)
    im = jnp.concatenate([x[:, s : s + width] for s in range(width, 2 * half, 2 * width)], axis=1)
    joined = jnp.concatenate([re, im, re, im], axis=0)
    spectra = dot_nn(forward[...], joined)
    points = x.shape[0]
    g_re, g_im = spectra[:points, : 2 * width], spectra[points:, : 2 * width]
    s_re, s_im = spectra[:points, 2 * width :], spectra[points:, 2 * width :]
    product = jnp.concatenate([g_re * s_re - g_im * s_im, g_re * s_im + g_im * s_re], axis=0)
    high = product.astype(BF16)
    rest = (product - high.astype(F32)).astype(BF16)
    table = inverse[...]
    back = dot_nn(table, jnp.concatenate([high, high], axis=0)) + dot_nn(
        table[:, : 2 * points], rest
    )
    result = back.astype(BF16)
    for b in range(2):
        for part in range(2):
            out[:, (2 * b + part) * width : (2 * b + part + 1) * width] = result[
                part * points : (part + 1) * points, b * width : (b + 1) * width
            ]


def unpack_kernel(packed, out):
    for b in range(2):
        for part in range(2):
            out[b, part] = unpack(packed[2 * b + part])


def call(kernel, out_shapes, specs, scratch=(), interpret=False):
    many = isinstance(out_shapes, (list, tuple))
    return pl.pallas_call(
        kernel,
        out_shape=out_shapes,
        in_specs=specs,
        out_specs=[VM] * len(out_shapes) if many else VM,
        scratch_shapes=scratch,
        interpret=interpret,
    )


def shape(*dims):
    return jax.ShapeDtypeStruct(dims, BF16)


def chip_groups(pairs):
    return [[2 * low + core, 2 * high + core] for low, high in pairs for core in range(2)]


def scan_blocks(green, coupling, screened, interpret=False):
    n = green.shape[-1]
    width = 6 * TILE
    index = lax.axis_index("space")
    place = jnp.stack([index // 4, index // 2 % 2, index % 2]).astype(jnp.int32)
    transfer, aggregate, screen = call(
        local_kernel,
        [shape(2, 2, n, n), shape(2, 2, n, n), shape(4, TILE, width)],
        [VM] * 3,
        interpret=interpret,
    )(green, coupling, screened)

    def gather(x, groups):
        return lax.all_gather(x, "space", axis_index_groups=groups)

    cores = gather(aggregate, [[2 * c, 2 * c + 1] for c in range(8)])
    chip = call(compose_kernel, shape(2, 2, n, n), [VM], interpret=interpret)(cores)
    chips = gather(chip, chip_groups([(0, 1), (2, 3), (4, 5), (6, 7)]))
    pair_map, end = call(
        pair_kernel, [shape(2, 2, n, n), shape(2, TILE, width)], [VM], interpret=interpret
    )(chips)
    prefix = jnp.zeros_like(end)
    odd = chip_groups([(0, 2), (1, 3), (4, 6), (5, 7)])
    even = chip_groups([(2, 4), (3, 5), (6, 0), (7, 1)])
    for hop in (1, 2):
        received = gather(end, odd if hop % 2 else even)
        end, prefix = call(
            lambda *refs, hop=hop: hop_kernel(hop, *refs),
            [shape(2, TILE, width), shape(2, TILE, width)],
            [SM] + [VM] * 4,
            interpret=interpret,
        )(place, received, pair_map, end, prefix)
    received = gather(end, odd)
    connected = call(
        lambda *refs: final_kernel(3, *refs),
        shape(4, TILE, width),
        [SM] + [VM] * 6,
        scratch=[pltpu.VMEM((2, n, n), BF16)],
        interpret=interpret,
    )(place, received, prefix, chips, cores, transfer, green)
    return connected, screen


def shards(iso_green, coupling, screened):
    points = lax.axis_size("energy")
    n = iso_green.shape[-1]
    width = 6 * TILE
    connected, screen = scan_blocks(iso_green[0], coupling, screened[0])
    sent = jnp.concatenate([connected, screen], axis=0).transpose(1, 0, 2).reshape(points, -1)
    values = lax.all_to_all(sent, "energy", split_axis=0, concat_axis=0, tiled=True)
    forward, inverse = tables(points)
    result = call(convolve_kernel, shape(points, 4 * width), [VM] * 3)(
        jnp.asarray(forward), jnp.asarray(inverse), values
    )
    returned = lax.all_to_all(result, "energy", split_axis=0, concat_axis=0, tiled=True)
    packed = returned.reshape(points, 4, width).transpose(1, 0, 2)
    return call(unpack_kernel, shape(2, 2, n, n), [VM])(packed)[None]


def solution(mesh):
    in_specs = (
        P("energy", "space", None, None, None),
        P("space", None, None),
        P("energy", "space", None, None, None),
    )
    out_specs = P("energy", "space", None, None, None)
    return jax.shard_map(shards, mesh=mesh, in_specs=in_specs, out_specs=out_specs, check_vma=False)
```

time: 226 us -> 140 us (0.62)
  the two profiles are of different devices: /device:TPU:14 before, /device:TPU:6 now
where the time goes in v1:
time: 140 us; the launch traced here: 139 us
  blocking collectives  107 us (76%)
  Pallas kernels  20.7 us (15%)
  other arithmetic  7.34 us (5%)
  local copies, waits for them, and re-layouts  4 us (3%)
    all_gather x5, blocking collectives, gather(): return lax.all_gather(x, 'space', axis_index_groups=groups)  55.1 us
    all_to_all x1, blocking collectives, shards(): lax.all_to_all(sent, 'energy', split_axis=0, concat_axis=0, tiled=True)  33.2 us
    all_to_all x1, blocking collectives, shards(): lax.all_to_all(result, 'energy', split_axis=0, concat_axis=0, tiled=True)  18.5 us
    pallas_call x2, Pallas kernels, scan_blocks(): call(lambda *refs, hop=hop: hop_kernel(hop, *refs), [shape(2, TILE, width...  4.52 us
    pallas_call x1, Pallas kernels, scan_blocks(): call(lambda *refs: final_kernel(3, *refs), shape(4, TILE, width), [SM] +...  4.19 us
    all_to_all x1, other arithmetic, shards(): lax.all_to_all(sent, 'energy', split_axis=0, concat_axis=0, tiled=True)  2.94 us
    pallas_call x1, Pallas kernels, scan_blocks(): call(local_kernel, [shape(2, 2, n, n), shape(2, 2, n, n), shape(4, TILE,...  2.8 us

profile of v1, /device:TPU:6, one launch (start us, length us, event | category | flops | bytes accessed | tf_op | source)
XLA Modules:
  0.0 138.9 jit_solution(3460444895491445926)
XLA Ops:
  0.0 2.8 %shard_map.55 = (bf16[2,2,192,192]{3,2,1,0:T(8,128)(2,1)}, bf16[2,2,192,192]{3,2,1,0:T(8,128)(2,1)}, bf16[4,64,384]{2,1,0:T(8,128)(2,1)}) custom-call(bf16[2,2,192,192]{3,2,1,0:T(8,128)(2,1)} %bitcast.28, bf16[2,192,192]{2,1,0:T(8,128)(2,1)} %coupling.1, bf16[2,2,192,192]{3,2,1,0:T(8,128)(2,1)} %bitcast.37), custom_call_target="tpu_custom_call" | custom-call | tf_op jit(solution)/shard_map/pallas_call | solution.py:218
  2.8 6.2 %all-gather = bf16[4,2,192,192]{3,2,1,0:T(8,128)(2,1)} all-gather(bf16[2,2,192,192]{3,2,1,0:T(8,128)(2,1)} %get-tuple-element.14), channel_id=2, replica_groups={{0,1},{2,3},{4,5},{6,7},{8,9},{10,11},{12,13},{14,15},{16,17},{18,19},{..., dimensions={0}, use_global_device_ids=true | all-gather | bytes 884736 | tf_op jit(solution)/shard_map/all_gather | solution.py:226
  9.0 2.5 %shard_map.56 = bf16[2,2,192,192]{3,2,1,0:T(8,128)(2,1)} custom-call(bf16[2,2,2,192,192]{4,3,2,1,0:T(8,128)(2,1)} %bitcast.24), custom_call_target="tpu_custom_call" | custom-call | tf_op jit(solution)/shard_map/pallas_call | solution.py:229
  11.4 14.9 %all-gather.1 = bf16[4,2,192,192]{3,2,1,0:T(8,128)(2,1)} all-gather(bf16[2,2,192,192]{3,2,1,0:T(8,128)(2,1)} %shard_map.56), channel_id=3, replica_groups={{0,2},{1,3},{4,6},{5,7},{8,10},{9,11},{12,14},{13,15},{16,18},{17,19},{..., dimensions={0}, use_global_device_ids=true | all-gather | bytes 884736 | tf_op jit(solution)/shard_map/all_gather | solution.py:226
  26.4 2.5 %shard_map.57 = (bf16[2,2,192,192]{3,2,1,0:T(8,128)(2,1)}, bf16[2,64,384]{2,1,0:T(8,128)(2,1)}) custom-call(bf16[2,2,2,192,192]{4,3,2,1,0:T(8,128)(2,1)} %bitcast.26), custom_call_target="tpu_custom_call" | custom-call | tf_op jit(solution)/shard_map/pallas_call | solution.py:231
  28.9 19.4 %all-gather.2 = bf16[4,64,384]{2,1,0:T(8,128)(2,1)} all-gather(bf16[2,64,384]{2,1,0:T(8,128)(2,1)} %get-tuple-element.15.refs_3_), channel_id=4, replica_groups={{0,4},{1,5},{2,6},{3,7},{8,12},{9,13},{10,14},{11,15},{16,20},{17,21},{..., dimensions={0}, use_global_device_ids=true | all-gather | bytes 294912 | tf_op jit(solution)/shard_map/all_gather | solution.py:226
  48.3 0.7 pad_add_fusion.refs_0_
  48.9 0.6 broadcast_in_dim.6.refs_4_
  49.6 2.7 %shard_map.58 = (bf16[2,64,384]{2,1,0:T(8,128)(2,1)}, bf16[2,64,384]{2,1,0:T(8,128)(2,1)}) custom-call(s32[3]{0:T(128)} %pad_add_fusion.refs_0_, bf16[2,2,64,384]{3,2,1,0:T(8,128)(2,1)} %bitcast.32, bf16[2,2,192,192]{3,2,1,0:T(8,128)(2,1)} %get-tuple-element.16.refs_2_, bf16[2,64,384]{2,1,0:T(8,128)(2,1)} %get-tuple-element.15.refs_3_, ...), custom_call_target="tpu_custom_call" | custom-call | tf_op jit(solution)/shard_map/pallas_call | solution.py:239
  52.2 7.8 %all-gather.3 = bf16[4,64,384]{2,1,0:T(8,128)(2,1)} all-gather(bf16[2,64,384]{2,1,0:T(8,128)(2,1)} %get-tuple-element.17.refs_3_), channel_id=5, replica_groups={{4,8},{5,9},{6,10},{7,11},{12,0},{13,1},{14,2},{15,3},{20,24},{21,25},{..., dimensions={0}, use_global_device_ids=true | all-gather | bytes 294912 | tf_op jit(solution)/shard_map/all_gather | solution.py:226
  60.1 1.8 %shard_map.59 = (bf16[2,64,384]{2,1,0:T(8,128)(2,1)}, bf16[2,64,384]{2,1,0:T(8,128)(2,1)}) custom-call(s32[3]{0:T(128)} %pad_add_fusion.refs_0_, bf16[2,2,64,384]{3,2,1,0:T(8,128)(2,1)} %bitcast.33, bf16[2,2,192,192]{3,2,1,0:T(8,128)(2,1)} %get-tuple-element.16.refs_2_, bf16[2,64,384]{2,1,0:T(8,128)(2,1)} %get-tuple-element.17.refs_3_, ...), custom_call_target="tpu_custom_call" | custom-call | tf_op jit(solution)/shard_map/pallas_call | solution.py:239
  61.9 6.8 %all-gather.4 = bf16[4,64,384]{2,1,0:T(8,128)(2,1)} all-gather(bf16[2,64,384]{2,1,0:T(8,128)(2,1)} %get-tuple-element.19), channel_id=6, replica_groups={{0,4},{1,5},{2,6},{3,7},{8,12},{9,13},{10,14},{11,15},{16,20},{17,21},{..., dimensions={0}, use_global_device_ids=true | all-gather | bytes 294912 | tf_op jit(solution)/shard_map/all_gather | solution.py:226
  68.7 0.0 copy-start
  68.7 4.2 %shard_map.60 = bf16[4,64,384]{2,1,0:T(8,128)(2,1)} custom-call(s32[3]{0:T(128)} %pad_add_fusion.refs_0_, bf16[2,2,64,384]{3,2,1,0:T(8,128)(2,1)} %bitcast.31, bf16[2,64,384]{2,1,0:T(8,128)(2,1)} %get-tuple-element.20.refs_2_, bf16[2,2,2,192,192]{4,3,2,1,0:T(8,128)(2,1)} %bitcast.27, bf16[2,2,2,192,192]{4,3,2,1,0:T(8,128)(2,1)} %bitcast.25, ...), custom_call_target="tpu_custom_call" | custom-call | tf_op jit(solution)/shard_map/pallas_call | solution.py:246
  72.9 0.0 copy-done
  72.9 1.0 maximum_bitcast_fusion
  73.8 0.2 copy.11
  74.1 0.2 all_to_all.18
  74.3 0.6 broadcast.5
  74.9 2.9 %reduce.1 = bf16[64,3072]{1,0:T(8,128)(2,1)S(1)} reduce(bf16[64,1,3072]{2,1,0:T(2,128)(2,1)S(1)} %all_to_all.18, bf16[]{:T(256)} %broadcast.5), dimensions={1}, to_apply=%all_to_all.18.reduce_sub_computation | reduce | bytes 786434 | tf_op jit(solution)/shard_map/all_to_all | solution.py:262
  77.8 0.3 reshape.17
  78.1 33.2 %all_to_all.21 = bf16[64,2,1536]{2,1,0:T(2,128)(2,1)S(1)} all-to-all(bf16[64,2,1536]{2,1,0:T(2,128)(2,1)S(1)} %reshape.17), channel_id=1, replica_groups=mesh['energy'=64,'space'=16] {'energy'}, dimensions={0} | all-to-all | bytes 786432 | tf_op jit(solution)/shard_map/all_to_all | solution.py:262
  111.3 0.3 reshape.18
  111.6 0.9 copy.19
  112.5 2.3 %shard_map.61 = bf16[64,1536]{1,0:T(8,128)(2,1)} custom-call(bf16[128,256]{1,0:T(8,128)(2,1)} %constant.48.clone.forward, bf16[128,256]{1,0:T(8,128)(2,1)} %constant.49.clone.inverse, bf16[64,3072]{1,0:T(8,128)(2,1)} %bitcast.30), custom_call_target="tpu_custom_call" | custom-call | tf_op jit(solution)/shard_map/pallas_call | solution.py:264
  114.8 1.6 %reduce.2 = bf16[64,1536]{1,0:T(8,128)(2,1)S(1)} reduce(bf16[64,1,1536]{2,0,1:T(8,128)(2,1)} %bitcast.34, bf16[]{:T(256)} %broadcast.5), dimensions={1}, to_apply=%copy.13.reduce_sub_computation | reduce | bytes 393218 | tf_op jit(solution)/shard_map/all_to_all | solution.py:267
  116.4 0.1 reshape.19
  116.5 18.5 %all_to_all.22 = bf16[64,2,768]{2,1,0:T(2,128)(2,1)S(1)} all-to-all(bf16[64,2,768]{2,1,0:T(2,128)(2,1)S(1)} %reshape.19), channel_id=1, replica_groups=mesh['energy'=64,'space'=16] {'energy'}, dimensions={0} | all-to-all | bytes 393216 | tf_op jit(solution)/shard_map/all_to_all | solution.py:267
  135.0 0.1 reshape.20
  135.1 1.1 reduce
  136.3 0.7 copy.20
  137.0 2.0 %shard_map.62 = bf16[2,2,192,192]{3,2,1,0:T(8,128)(2,1)} custom-call(bf16[4,64,384]{2,1,0:T(8,128)(2,1)} %bitcast.36), custom_call_target="tpu_custom_call" | custom-call | tf_op jit(solution)/shard_map/pallas_call | solution.py:269
Async XLA Ops:
  68.7 4.2 %copy-start = (bf16[4,64,384]{2,1,0:T(8,128)(2,1)S(1)}, bf16[4,64,384]{2,1,0:T(8,128)(2,1)}, u32[]{:S(2)}) copy-start(bf16[4,64,384]{2,1,0:T(8,128)(2,1)} %get-tuple-element.22) | copy-start | bytes 589828

commit v2 on v1

--- a/solution.py
+++ b/solution.py
@@ -11,9 +11,9 @@
 F32 = jnp.float32
 BF16 = jnp.bfloat16
 TILE = 64
+VMEM_GRANT = 16 * 2**20
 
 VM = pl.BlockSpec(memory_space=pltpu.VMEM)
-SM = pl.BlockSpec(memory_space=pltpu.SMEM)
 
 
 def dot_nn(a, b):
@@ -65,7 +65,7 @@
     ref[(*at, 1)] = pair[1]
 
 
-def local_kernel(green, coupling, screened, transfer, aggregate, packed):
+def local_kernel(green, coupling, transfer, aggregate):
     maps = []
     for b in range(2):
         k = coupling[b]
@@ -76,9 +76,6 @@
     (t0, g0), (t1, g1) = maps
     store(aggregate, rounded(complex_product(t1, t0, dot_nn)), 0)
     store(aggregate, sandwich(g0, t1, g1), 1)
-    for b in range(2):
-        for part in range(2):
-            packed[2 * b + part] = pack(screened[b, part])
 
 
 def compose_kernel(pairs, out):
@@ -88,7 +85,8 @@
     store(out, sandwich(low[1], high[0], high[1]), 1)
 
 
-def pair_kernel(pairs, out, end):
+def pair_kernel(pairs, screened, out, end, prefix, screen):
+    prefix[...] = jnp.zeros(prefix.shape, BF16)
     low = load(pairs, 0, 0), load(pairs, 0, 1)
     high = load(pairs, 1, 0), load(pairs, 1, 1)
     store(out, rounded(complex_product(high[0], low[0], dot_nn)), 0)
@@ -96,10 +94,14 @@
     store(out, c, 1)
     end[0] = pack(c[0])
     end[1] = pack(c[1])
-
-
-def hop_kernel(hop, place, received, pair_map, end_in, prefix_in, end, prefix):
-    mine = place[0] == hop
+    for b in range(2):
+        for part in range(2):
+            screen[2 * b + part] = pack(screened[b, part])
+
+
+def hop_kernel(hop, received, pair_map, end_in, prefix_in, end, prefix):
+    index = lax.axis_index("space")
+    mine = index // 4 == hop
 
     @pl.when(mine)
     def _():
@@ -115,8 +117,13 @@
         prefix[...] = prefix_in[...]
 
 
-def final_kernel(hop, place, received, prefix_in, chips, cores, transfer, green, packed, state):
-    mine = place[0] == hop
+def rows_first(parts):
+    return jnp.swapaxes(jnp.stack([p.astype(F32) for p in parts], axis=0), 0, 1).astype(BF16)
+
+
+def final_kernel(hop, received, prefix_in, chips, cores, transfer, green, screen, sent, state):
+    index = lax.axis_index("space")
+    mine = index // 4 == hop
 
     @pl.when(mine)
     def _():
@@ -128,19 +135,20 @@
         state[0] = unpack(prefix_in[0])
         state[1] = unpack(prefix_in[1])
 
-    @pl.when(place[1] == 1)
+    @pl.when(index // 2 % 2 == 1)
     def _():
         store(state, sandwich(load(state), load(chips, 0, 0), load(chips, 0, 1)))
 
-    @pl.when(place[2] == 1)
+    @pl.when(index % 2 == 1)
     def _():
         store(state, sandwich(load(state), load(cores, 0, 0), load(cores, 0, 1)))
 
     carried = load(state)
+    parts = []
     for b in range(2):
         carried = sandwich(carried, load(transfer, b), load(green, b))
-        packed[2 * b] = pack(carried[0])
-        packed[2 * b + 1] = pack(carried[1])
+        parts += [pack(carried[0]), pack(carried[1])]
+    sent[...] = rows_first(parts + [screen[j] for j in range(4)])
 
 
 def split(table):
@@ -159,14 +167,12 @@
 
 
 def convolve_kernel(forward, inverse, values, out):
-    half = values.shape[1] // 2
-    width = half // 4
-    x = values[...]
-    re = jnp.concatenate([x[:, s : s + width] for s in range(0, 2 * half, 2 * width)], axis=1)
-    im = jnp.concatenate([x[:, s : s + width] for s in range(width, 2 * half, 2 * width)], axis=1)
+    points, _, width = values.shape
+    x = jnp.swapaxes(values[...].astype(F32), 0, 1).astype(BF16)
+    re = jnp.concatenate([x[j] for j in (0, 2, 4, 6)], axis=1)
+    im = jnp.concatenate([x[j] for j in (1, 3, 5, 7)], axis=1)
     joined = jnp.concatenate([re, im, re, im], axis=0)
     spectra = dot_nn(forward[...], joined)
-    points = x.shape[0]
     g_re, g_im = spectra[:points, : 2 * width], spectra[points:, : 2 * width]
     s_re, s_im = spectra[:points, 2 * width :], spectra[points:, 2 * width :]
     product = jnp.concatenate([g_re * s_re - g_im * s_im, g_re * s_im + g_im * s_re], axis=0)
@@ -176,18 +182,20 @@
     back = dot_nn(table, jnp.concatenate([high, high], axis=0)) + dot_nn(
         table[:, : 2 * points], rest
     )
-    result = back.astype(BF16)
+    out[...] = rows_first(
+        [
+            back[part * points : (part + 1) * points, b * width : (b + 1) * width]
+            for b in range(2)
+            for part in range(2)
+        ]
+    )
+
+
+def unpack_kernel(packed, out):
+    parts = jnp.swapaxes(packed[...].astype(F32), 0, 1)
     for b in range(2):
         for part in range(2):
-            out[:, (2 * b + part) * width : (2 * b + part + 1) * width] = result[
-                part * points : (part + 1) * points, b * width : (b + 1) * width
-            ]
-
-
-def unpack_kernel(packed, out):
-    for b in range(2):
-        for part in range(2):
-            out[b, part] = unpack(packed[2 * b + part])
+            out[b, part] = unpack(parts[2 * b + part])
 
 
 def call(kernel, out_shapes, specs, scratch=(), interpret=False):
@@ -198,6 +206,7 @@
         in_specs=specs,
         out_specs=[VM] * len(out_shapes) if many else VM,
         scratch_shapes=scratch,
+        compiler_params=pltpu.CompilerParams(vmem_limit_bytes=VMEM_GRANT),
         interpret=interpret,
     )
 
@@ -213,14 +222,9 @@
 def scan_blocks(green, coupling, screened, interpret=False):
     n = green.shape[-1]
     width = 6 * TILE
-    index = lax.axis_index("space")
-    place = jnp.stack([index // 4, index // 2 % 2, index % 2]).astype(jnp.int32)
-    transfer, aggregate, screen = call(
-        local_kernel,
-        [shape(2, 2, n, n), shape(2, 2, n, n), shape(4, TILE, width)],
-        [VM] * 3,
-        interpret=interpret,
-    )(green, coupling, screened)
+    transfer, aggregate = call(
+        local_kernel, [shape(2, 2, n, n), shape(2, 2, n, n)], [VM] * 2, interpret=interpret
+    )(green, coupling)
 
     def gather(x, groups):
         return lax.all_gather(x, "space", axis_index_groups=groups)
@@ -228,45 +232,44 @@
     cores = gather(aggregate, [[2 * c, 2 * c + 1] for c in range(8)])
     chip = call(compose_kernel, shape(2, 2, n, n), [VM], interpret=interpret)(cores)
     chips = gather(chip, chip_groups([(0, 1), (2, 3), (4, 5), (6, 7)]))
-    pair_map, end = call(
-        pair_kernel, [shape(2, 2, n, n), shape(2, TILE, width)], [VM], interpret=interpret
-    )(chips)
-    prefix = jnp.zeros_like(end)
-    odd = chip_groups([(0, 2), (1, 3), (4, 6), (5, 7)])
-    even = chip_groups([(2, 4), (3, 5), (6, 0), (7, 1)])
+    pair_map, end, prefix, screen = call(
+        pair_kernel,
+        [shape(2, 2, n, n)] + [shape(2, TILE, width)] * 2 + [shape(4, TILE, width)],
+        [VM] * 2,
+        interpret=interpret,
+    )(chips, screened)
+    outer = chip_groups([(0, 2), (1, 3), (4, 6), (5, 7)])
+    inner = chip_groups([(0, 1), (2, 4), (3, 5), (6, 7)])
     for hop in (1, 2):
-        received = gather(end, odd if hop % 2 else even)
+        received = gather(end, outer if hop % 2 else inner)
         end, prefix = call(
             lambda *refs, hop=hop: hop_kernel(hop, *refs),
             [shape(2, TILE, width), shape(2, TILE, width)],
-            [SM] + [VM] * 4,
+            [VM] * 4,
             interpret=interpret,
-        )(place, received, pair_map, end, prefix)
-    received = gather(end, odd)
-    connected = call(
+        )(received, pair_map, end, prefix)
+    received = gather(end, outer)
+    return call(
         lambda *refs: final_kernel(3, *refs),
-        shape(4, TILE, width),
-        [SM] + [VM] * 6,
+        shape(TILE, 8, width),
+        [VM] * 7,
         scratch=[pltpu.VMEM((2, n, n), BF16)],
         interpret=interpret,
-    )(place, received, prefix, chips, cores, transfer, green)
-    return connected, screen
+    )(received, prefix, chips, cores, transfer, green, screen)
 
 
 def shards(iso_green, coupling, screened):
     points = lax.axis_size("energy")
     n = iso_green.shape[-1]
     width = 6 * TILE
-    connected, screen = scan_blocks(iso_green[0], coupling, screened[0])
-    sent = jnp.concatenate([connected, screen], axis=0).transpose(1, 0, 2).reshape(points, -1)
+    sent = scan_blocks(iso_green[0], coupling, screened[0])
     values = lax.all_to_all(sent, "energy", split_axis=0, concat_axis=0, tiled=True)
     forward, inverse = tables(points)
-    result = call(convolve_kernel, shape(points, 4 * width), [VM] * 3)(
+    result = call(convolve_kernel, shape(points, 4, width), [VM] * 3)(
         jnp.asarray(forward), jnp.asarray(inverse), values
     )
     returned = lax.all_to_all(result, "energy", split_axis=0, concat_axis=0, tiled=True)
-    packed = returned.reshape(points, 4, width).transpose(1, 0, 2)
-    return call(unpack_kernel, shape(2, 2, n, n), [VM])(packed)[None]
+    return call(unpack_kernel, shape(2, 2, n, n), [VM])(returned)[None]
 
 
 def solution(mesh):

time: 140 us -> 101 us (0.72)
  blocking collectives: 107 us -> 91.7 us
  Pallas kernels: 20.7 us -> 6.54 us
  other arithmetic: 7.34 us -> 0 us
  local copies, waits for them, and re-layouts: 4 us -> 1.95 us
    all_gather x5, blocking collectives: 55.1 us -> 45.4 us  [gather(): return lax.all_gather(x, 'space', axis_index_groups=groups)]
    pallas_call x5, Pallas kernels: 13.7 us -> 5.08 us  [the longest x1 1.87 us: scan_blocks(): call(lambda *refs: final_kernel(3, *refs), shape(TILE, 8, width), [VM] *...]
    all_to_all x3 -> x0, other arithmetic: 5.71 us -> none  [the longest x1 2.94 us: shards(): lax.all_to_all(sent, 'energy', split_axis=0, concat_axis=0, tiled=True)]
    all_to_all x1, blocking collectives: 33.2 us -> 28.9 us  [shards(): lax.all_to_all(sent, 'energy', split_axis=0, concat_axis=0, tiled=True)]
    pallas_call x2, Pallas kernels: 4.52 us -> 0.87 us  [scan_blocks(): call(lambda *refs, hop=hop: hop_kernel(hop, *refs), [shape(2, TILE, width...]
    pallas_call x1, Pallas kernels: 2.47 us -> 0.59 us  [scan_blocks(): call(compose_kernel, shape(2, 2, n, n), [VM], interpret=interpret)(cores)]
where the time goes in v2:
time: 101 us; the launch traced here: 100 us
  blocking collectives  91.7 us (91%)
  Pallas kernels  6.54 us (6%)
  local copies, waits for them, and re-layouts  1.95 us (2%)
    all_gather x5, blocking collectives, gather(): return lax.all_gather(x, 'space', axis_index_groups=groups)  45.4 us
    all_to_all x1, blocking collectives, shards(): lax.all_to_all(sent, 'energy', split_axis=0, concat_axis=0, tiled=True)  28.9 us
    all_to_all x1, blocking collectives, shards(): lax.all_to_all(result, 'energy', split_axis=0, concat_axis=0, tiled=True)  17.5 us

profile of v2, /device:TPU:6, one launch (start us, length us, event | category | flops | bytes accessed | tf_op | source)
XLA Modules:
  0.0 100.3 jit_solution(18210107481301254590)
XLA Ops:
  0.0 0.0 copy-start
  0.0 1.0 copy-done
  1.0 0.0 copy-start.3
  1.0 0.9 copy-done.3
  1.9 0.8 shard_map.55
  2.7 2.4 %all-gather = bf16[4,2,192,192]{3,2,1,0:T(8,128)(2,1)S(1)} all-gather(bf16[2,2,192,192]{3,2,1,0:T(8,128)(2,1)S(1)} %get-tuple-element.15), channel_id=2, replica_groups={{0,1},{2,3},{4,5},{6,7},{8,9},{10,11},{12,13},{14,15},{16,17},{18,19},{..., dimensions={0}, use_global_device_ids=true | all-gather | bytes 884736 | tf_op jit(solution)/shard_map/all_gather | solution.py:230
  5.1 0.6 shard_map.56
  5.7 0.0 copy-start.2
  5.7 12.3 %all-gather.1 = bf16[4,2,192,192]{3,2,1,0:T(8,128)(2,1)S(1)} all-gather(bf16[2,2,192,192]{3,2,1,0:T(8,128)(2,1)S(1)} %shard_map.56), channel_id=3, replica_groups={{0,2},{1,3},{4,6},{5,7},{8,10},{9,11},{12,14},{13,15},{16,18},{17,19},{..., dimensions={0}, use_global_device_ids=true | all-gather | bytes 884736 | tf_op jit(solution)/shard_map/all_gather | solution.py:230
  18.0 0.0 copy-done.2
  18.0 0.7 shard_map.57
  18.7 16.8 %all-gather.2 = bf16[4,64,384]{2,1,0:T(8,128)(2,1)S(1)} all-gather(bf16[2,64,384]{2,1,0:T(8,128)(2,1)S(1)} %get-tuple-element.16.refs_2_), channel_id=4, replica_groups={{0,4},{1,5},{2,6},{3,7},{8,12},{9,13},{10,14},{11,15},{16,20},{17,21},{..., dimensions={0}, use_global_device_ids=true | all-gather | bytes 294912 | tf_op jit(solution)/shard_map/all_gather | solution.py:230
  35.5 0.8 shard_map.58
  36.4 7.5 %all-gather.3 = bf16[4,64,384]{2,1,0:T(8,128)(2,1)S(1)} all-gather(bf16[2,64,384]{2,1,0:T(8,128)(2,1)S(1)} %get-tuple-element.19.refs_2_), channel_id=5, replica_groups={{0,2},{1,3},{4,8},{5,9},{6,10},{7,11},{12,14},{13,15},{16,18},{17,19},{..., dimensions={0}, use_global_device_ids=true | all-gather | bytes 294912 | tf_op jit(solution)/shard_map/all_gather | solution.py:230
  43.9 0.0 copy-start.1
  43.9 6.3 %all-gather.4 = bf16[4,64,384]{2,1,0:T(8,128)(2,1)S(1)} all-gather(bf16[2,64,384]{2,1,0:T(8,128)(2,1)S(1)} %get-tuple-element.21), channel_id=6, replica_groups={{0,4},{1,5},{2,6},{3,7},{8,12},{9,13},{10,14},{11,15},{16,20},{17,21},{..., dimensions={0}, use_global_device_ids=true | all-gather | bytes 294912 | tf_op jit(solution)/shard_map/all_gather | solution.py:230
  50.2 0.0 copy-done.1
  50.2 1.9 %shard_map.60 = bf16[64,8,384]{2,1,0:T(8,128)(2,1)S(1)} custom-call(bf16[2,2,64,384]{3,2,1,0:T(8,128)(2,1)S(1)} %bitcast.14, bf16[2,64,384]{2,1,0:T(8,128)(2,1)S(1)} %get-tuple-element.22.refs_1_, bf16[2,2,2,192,192]{4,3,2,1,0:T(8,128)(2,1)S(1)} %bitcast.11, bf16[2,2,2,192,192]{4,3,2,1,0:T(8,128)(2,1)S(1)} %bitcast.9, ...), custom_call_target="tpu_custom_call" | custom-call | tf_op jit(solution)/shard_map/pallas_call | solution.py:252
  52.1 0.0 copy-start.4
  52.1 0.0 copy-start.5
  52.1 28.9 %all_to_all.10.values = bf16[64,8,384]{2,1,0:T(8,128)(2,1)S(1)} all-to-all(bf16[64,8,384]{2,1,0:T(8,128)(2,1)S(1)} %shard_map.60), channel_id=1, replica_groups=mesh['energy'=64,'space'=16] {'energy'}, dimensions={0} | all-to-all | bytes 786432 | tf_op jit(solution)/shard_map/all_to_all | solution.py:266
  81.0 0.0 copy-done.4
  81.0 0.0 copy-done.5
  81.0 0.7 shard_map.61
  81.8 17.5 %all_to_all.11.packed = bf16[64,4,384]{2,1,0:T(4,128)(2,1)S(1)} all-to-all(bf16[64,4,384]{2,1,0:T(4,128)(2,1)S(1)} %shard_map.61), channel_id=1, replica_groups=mesh['energy'=64,'space'=16] {'energy'}, dimensions={0} | all-to-all | bytes 393216 | tf_op jit(solution)/shard_map/all_to_all | solution.py:271
  99.2 1.0 %shard_map.62 = bf16[2,2,192,192]{3,2,1,0:T(8,128)(2,1)} custom-call(bf16[64,4,384]{2,1,0:T(4,128)(2,1)S(1)} %all_to_all.11.packed), custom_call_target="tpu_custom_call" | custom-call | tf_op jit(solution)/shard_map/pallas_call | solution.py:272
  (1 shorter events, 0.0 us)
Async XLA Ops:
  0.0 1.0 copy-start
  1.0 0.9 copy-start.3
  5.7 12.4 %copy-start.2 = (bf16[1,2,2,192,192]{4,3,2,1,0:T(8,128)(2,1)S(1)}, bf16[1,2,2,192,192]{4,3,2,1,0:T(8,128)(2,1)}, u32[]{:S(2)}) copy-start(bf16[1,2,2,192,192]{4,3,2,1,0:T(8,128)(2,1)} %param.7) | copy-start | bytes 884740
  43.9 6.3 %copy-start.1 = (bf16[1,2,2,192,192]{4,3,2,1,0:T(8,128)(2,1)S(1)}, bf16[1,2,2,192,192]{4,3,2,1,0:T(8,128)(2,1)}, u32[]{:S(2)}) copy-start(bf16[1,2,2,192,192]{4,3,2,1,0:T(8,128)(2,1)} %param.5) | copy-start | bytes 884740
  52.1 28.9 %copy-start.4 = (bf16[128,256]{1,0:T(8,128)(2,1)S(1)}, bf16[128,256]{1,0:T(8,128)(2,1)}, u32[]{:S(2)}) copy-start(bf16[128,256]{1,0:T(8,128)(2,1)} %constant.5.clone.inverse) | copy-start | bytes 196612
  52.1 28.9 %copy-start.5 = (bf16[128,256]{1,0:T(8,128)(2,1)S(1)}, bf16[128,256]{1,0:T(8,128)(2,1)}, u32[]{:S(2)}) copy-start(bf16[128,256]{1,0:T(8,128)(2,1)} %constant.4.clone.forward) | copy-start | bytes 196612

commit v3 on v2

v3 whole, which is shorter than its diff:
```python
import math

import jax
import jax.numpy as jnp
import numpy as np
from jax import lax
from jax.experimental import pallas as pl
from jax.experimental.pallas import tpu as pltpu
from jax.sharding import PartitionSpec as P

F32 = jnp.float32
BF16 = jnp.bfloat16
TILE = 64
PACKED = 5 * TILE
MAP = 14 * TILE
VMEM_GRANT = 16 * 2**20

VM = pl.BlockSpec(memory_space=pltpu.VMEM)
HB = pl.BlockSpec(memory_space=pltpu.HBM)


def dot_nn(a, b):
    return lax.dot_general(a, b, (((1,), (0,)), ((), ())), preferred_element_type=F32)


def dot_nt(a, b):
    return lax.dot_general(a, b, (((1,), (1,)), ((), ())), preferred_element_type=F32)


def complex_product(a, b, dot):
    a_re, a_im = a
    b_re, b_im = b
    return dot(a_re, b_re) - dot(a_im, b_im), dot(a_re, b_im) + dot(a_im, b_re)


def rounded(pair):
    return pair[0].astype(BF16), pair[1].astype(BF16)


def sandwich(carried, factor, source):
    middle = rounded(complex_product(carried, factor, dot_nt))
    re, im = complex_product(factor, middle, dot_nn)
    return rounded((source[0].astype(F32) + re, source[1].astype(F32) + im))


def half_turn(x):
    return pltpu.roll(x, TILE, 1)


def place_of(shape):
    row = lax.broadcasted_iota(jnp.int32, shape, 0)
    col = lax.broadcasted_iota(jnp.int32, shape, 1)
    return row, col


def widened(x):
    return jnp.concatenate([x, x], axis=1)


def pack(m):
    t = TILE
    m = m.astype(F32)
    row, col = place_of((t, 2 * t))
    top, mid = m[:t, : 2 * t], m[t : 2 * t, : 2 * t]
    right = [widened(m[k * t : (k + 1) * t, 2 * t :]) for k in range(3)]
    left = col < t
    d1 = jnp.where(col == row + t, mid, 0.0)
    diagonal = jnp.sum(d1, axis=1, keepdims=True)
    spare = jnp.where(col == 0, diagonal, jnp.where((row == 2) & (col == 1), diagonal[:1], 0.0))
    shared = jnp.where(col - t >= row, half_turn(top), mid)
    last = jnp.where(col >= row, right[2], spare)
    return jnp.where(left, right[0], top), jnp.where(left, right[1], shared), last


def unpack(first, second, y):
    t = TILE
    row, col = place_of((t, 2 * t))
    left = col < t
    first_t, second_t = first.T, second.T
    t02, t01, t12, x_t = first_t[:t], first_t[t:], second_t[:t], second_t[t:]
    diagonal = jnp.where(row[:, :1] == 0, y[2:3, 1:2], y[:, :1])
    d0 = jnp.where(col >= row, half_turn(second), widened(x_t))
    d1 = jnp.where(
        col - t < row, second, jnp.where(col - t > row, widened(x_t), diagonal)
    )
    d2 = jnp.where((col >= row)[:, :t], y[:, :t], y[:, :t].T)
    wide = [
        jnp.where(left, d0, first),
        jnp.where(left, widened(t01), d1),
        jnp.where(left, widened(t02), widened(t12)),
    ]
    narrow = [first[:, :t], second[:, :t], d2]
    return jnp.concatenate(
        [jnp.concatenate(wide, axis=0), jnp.concatenate(narrow, axis=0)], axis=1
    ).astype(BF16)


def pack_pair(pair):
    (a_re, b_re, c_re), (a_im, b_im, c_im) = pack(pair[0]), pack(pair[1])
    _, col = place_of(c_re.shape)
    last = jnp.where(col < TILE, c_re, half_turn(c_im))
    return jnp.concatenate([a_re, b_re, a_im, b_im, last], axis=1)


def unpack_pair(p):
    p = p.astype(F32)
    parts = [p[:, 2 * TILE * k : 2 * TILE * (k + 1)] for k in range(5)]
    return unpack(parts[0], parts[1], parts[4]), unpack(parts[2], parts[3], half_turn(parts[4]))


def store_map(ref, a, c):
    n, w = 3 * TILE, 2 * TILE
    ref[:n] = a[0][:, :w]
    ref[n : 2 * n] = a[1][:, :w]
    ref[2 * n : 3 * n] = jnp.concatenate([a[0][:, w:], a[1][:, w:]], axis=1)
    packed = pack_pair(c).astype(BF16)
    for k in range(5):
        ref[3 * n + k * TILE : 3 * n + (k + 1) * TILE] = packed[:, k * w : (k + 1) * w]


def load_map(ref):
    n, w = 3 * TILE, 2 * TILE
    rest = ref[2 * n : 3 * n]
    a = (
        jnp.concatenate([ref[:n], rest[:, :TILE]], axis=1),
        jnp.concatenate([ref[n : 2 * n], rest[:, TILE:]], axis=1),
    )
    packed = [ref[3 * n + k * TILE : 3 * n + (k + 1) * TILE] for k in range(5)]
    return a, unpack_pair(jnp.concatenate(packed, axis=1))


def load(ref, *at):
    return ref[(*at, 0)], ref[(*at, 1)]


def store(ref, pair, *at):
    ref[(*at, 0)] = pair[0]
    ref[(*at, 1)] = pair[1]


def local_kernel(green, coupling, transfer, aggregate, green_in, coupling_in, arrived):
    copies = [
        (
            pltpu.make_async_copy(coupling.at[b], coupling_in.at[b], arrived.at[b, 0]),
            pltpu.make_async_copy(green.at[b, 0], green_in.at[b, 0], arrived.at[b, 1]),
            pltpu.make_async_copy(green.at[b, 1], green_in.at[b, 1], arrived.at[b, 2]),
        )
        for b in range(2)
    ]
    for block in copies:
        for copy in block:
            copy.start()
    maps = []
    for b in range(2):
        for copy in copies[b]:
            copy.wait()
        k = coupling_in[b]
        g = load(green_in, b)
        t = rounded((dot_nn(g[0], k), dot_nn(g[1], k)))
        store(transfer, t, b)
        maps.append((t, g))
    (t0, g0), (t1, g1) = maps
    store_map(aggregate, rounded(complex_product(t1, t0, dot_nn)), sandwich(g0, t1, g1))


def joined(maps):
    (a_low, c_low), (a_high, c_high) = load_map(maps.at[0]), load_map(maps.at[1])
    return rounded(complex_product(a_high, a_low, dot_nn)), sandwich(c_low, a_high, c_high)


def compose_kernel(maps, out):
    store_map(out, *joined(maps))


def pair_kernel(maps, screened, out, end, prefix, screen):
    prefix[...] = jnp.zeros(prefix.shape, BF16)
    a, c = joined(maps)
    store(out, a, 0)
    store(out, c, 1)
    end[...] = pack_pair(c).astype(BF16)
    for b in range(2):
        screen[b] = pack_pair(load(screened, b)).astype(BF16)


def hop_kernel(hop, received, pair_map, end_in, prefix_in, end, prefix):
    mine = lax.axis_index("space") // 4 == hop

    @pl.when(mine)
    def _():
        before = unpack_pair(received[0])
        end[...] = pack_pair(sandwich(before, load(pair_map, 0), load(pair_map, 1))).astype(BF16)
        prefix[...] = received[0]

    @pl.when(jnp.logical_not(mine))
    def _():
        end[...] = end_in[...]
        prefix[...] = prefix_in[...]


def rows_first(parts):
    return jnp.swapaxes(jnp.stack([p.astype(F32) for p in parts], axis=0), 0, 1).astype(BF16)


def final_kernel(hop, received, prefix_in, chips, cores, transfer, green, screen, sent, state):
    index = lax.axis_index("space")
    mine = index // 4 == hop

    @pl.when(mine)
    def _():
        store(state, unpack_pair(received[0]))

    @pl.when(jnp.logical_not(mine))
    def _():
        store(state, unpack_pair(prefix_in[...]))

    @pl.when(index // 2 % 2 == 1)
    def _():
        store(state, sandwich(load(state), *load_map(chips.at[0])))

    @pl.when(index % 2 == 1)
    def _():
        store(state, sandwich(load(state), *load_map(cores.at[0])))

    carried = load(state)
    parts = []
    for b in range(2):
        carried = sandwich(carried, load(transfer, b), load(green, b))
        parts.append(pack_pair(carried))
    sent[...] = rows_first(parts + [screen[0], screen[1]])


def split(table):
    high = table.astype(jnp.bfloat16)
    return high, (table - high.astype(np.float32)).astype(jnp.bfloat16)


def tables(points):
    row = np.arange(points)
    angles = (row[:, None] * row[None, :] % points) * (2.0 * math.pi / points)
    cos, sin = np.cos(angles), np.sin(angles)
    forward = np.block([[cos, sin], [-sin, cos]]).astype(np.float32)
    scaling = 1.0 / (points * math.sqrt(points))
    inverse = (np.block([[-sin, -cos], [cos, -sin]]) * scaling).astype(np.float32)
    return np.concatenate(split(forward), axis=1), np.concatenate(split(inverse), axis=1)


def convolve_kernel(forward, inverse, values, out):
    points, _, lanes = values.shape
    part = 4 * TILE
    x = jnp.swapaxes(values[...].astype(F32), 0, 1)
    _, col = place_of((points, 2 * TILE))
    left = col < TILE

    def mixed(first, second):
        return jnp.where(left, first, half_turn(second)), jnp.where(left, half_turn(first), second)

    re, im = [], []
    for k in (0, 2):
        last_re, last_im = mixed(x[k, :, 2 * part :], x[k + 1, :, 2 * part :])
        re += [x[k, :, :part], x[k + 1, :, :part], last_re]
        im += [x[k, :, part : 2 * part], x[k + 1, :, part : 2 * part], last_im]
    re = jnp.concatenate(re, axis=1).astype(BF16)
    im = jnp.concatenate(im, axis=1).astype(BF16)
    spectra = dot_nn(forward[...], jnp.concatenate([re, im, re, im], axis=0))
    g_re, g_im = spectra[:points, :lanes], spectra[points:, :lanes]
    s_re, s_im = spectra[:points, lanes:], spectra[points:, lanes:]
    product = jnp.concatenate([g_re * s_re - g_im * s_im, g_re * s_im + g_im * s_re], axis=0)
    high = product.astype(BF16)
    rest = (product - high.astype(F32)).astype(BF16)
    table = inverse[...]
    back = dot_nn(table, jnp.concatenate([high, high], axis=0)) + dot_nn(
        table[:, : 2 * points], rest
    )
    b_re, b_im = back[:points], back[points:]
    last = mixed(b_re[:, 2 * part :], b_im[:, 2 * part :])
    out[...] = rows_first(
        [
            jnp.concatenate(
                [b_re[:, b * part : (b + 1) * part], b_im[:, b * part : (b + 1) * part], last[b]],
                axis=1,
            )
            for b in range(2)
        ]
    )


def unpack_kernel(packed, out, block, left):
    parts = jnp.swapaxes(packed[...].astype(F32), 0, 1)
    copies = []
    for b in range(2):
        store(block, unpack_pair(parts[b]), b)
        copies.append(pltpu.make_async_copy(block.at[b], out.at[b], left.at[b]))
        copies[b].start()
    for copy in copies:
        copy.wait()


def call(kernel, out_shapes, specs, scratch=(), interpret=False, out_spec=VM):
    many = isinstance(out_shapes, (list, tuple))
    return pl.pallas_call(
        kernel,
        out_shape=out_shapes,
        in_specs=specs,
        out_specs=[out_spec] * len(out_shapes) if many else out_spec,
        scratch_shapes=scratch,
        compiler_params=pltpu.CompilerParams(vmem_limit_bytes=VMEM_GRANT),
        interpret=interpret,
    )


def shape(*dims):
    return jax.ShapeDtypeStruct(dims, BF16)


def chip_groups(pairs):
    return [[2 * low + core, 2 * high + core] for low, high in pairs for core in range(2)]


def scan_blocks(green, coupling, screened, interpret=False):
    n = green.shape[-1]
    transfer, aggregate = call(
        local_kernel,
        [shape(2, 2, n, n), shape(MAP, 2 * TILE)],
        [HB] * 2,
        scratch=[
            pltpu.VMEM((2, 2, n, n), BF16),
            pltpu.VMEM((2, n, n), BF16),
            pltpu.SemaphoreType.DMA((2, 3)),
        ],
        interpret=interpret,
    )(green, coupling)

    def gather(x, groups):
        return lax.all_gather(x, "space", axis_index_groups=groups)

    cores = gather(aggregate, [[2 * c, 2 * c + 1] for c in range(8)])
    chip = call(compose_kernel, shape(MAP, 2 * TILE), [VM], interpret=interpret)(cores)
    chips = gather(chip, chip_groups([(0, 1), (2, 3), (4, 5), (6, 7)]))
    pair_map, end, prefix, screen = call(
        pair_kernel,
        [shape(2, 2, n, n)] + [shape(TILE, 2 * PACKED)] * 2 + [shape(2, TILE, 2 * PACKED)],
        [VM] * 2,
        interpret=interpret,
    )(chips, screened)
    outer = chip_groups([(0, 2), (1, 3), (4, 6), (5, 7)])
    inner = chip_groups([(0, 1), (2, 4), (3, 5), (6, 7)])
    for hop in (1, 2):
        received = gather(end, outer if hop % 2 else inner)
        end, prefix = call(
            lambda *refs, hop=hop: hop_kernel(hop, *refs),
            [shape(TILE, 2 * PACKED)] * 2,
            [VM] * 4,
            interpret=interpret,
        )(received, pair_map, end, prefix)
    received = gather(end, outer)
    return call(
        lambda *refs: final_kernel(3, *refs),
        shape(TILE, 4, 2 * PACKED),
        [VM] * 7,
        scratch=[pltpu.VMEM((2, n, n), BF16)],
        interpret=interpret,
    )(received, prefix, chips, cores, transfer, green, screen)


def shards(iso_green, coupling, screened):
    points = lax.axis_size("energy")
    n = iso_green.shape[-1]
    sent = scan_blocks(iso_green[0], coupling, screened[0])
    values = lax.all_to_all(sent, "energy", split_axis=0, concat_axis=0, tiled=True)
    forward, inverse = tables(points)
    result = call(convolve_kernel, shape(points, 2, 2 * PACKED), [VM] * 3)(
        jnp.asarray(forward), jnp.asarray(inverse), values
    )
    returned = lax.all_to_all(result, "energy", split_axis=0, concat_axis=0, tiled=True)
    return call(
        unpack_kernel,
        shape(2, 2, n, n),
        [VM],
        scratch=[pltpu.VMEM((2, 2, n, n), BF16), pltpu.SemaphoreType.DMA((2,))],
        out_spec=HB,
    )(returned)[None]


def solution(mesh):
    in_specs = (
        P("energy", "space", None, None, None),
        P("space", None, None),
        P("energy", "space", None, None, None),
    )
    out_specs = P("energy", "space", None, None, None)
    return jax.shard_map(shards, mesh=mesh, in_specs=in_specs, out_specs=out_specs, check_vma=False)
```

time: 101 us -> 97.3 us (0.963)
  the two profiles are of different devices: /device:TPU:6 before, /device:TPU:14 now
where the time goes in v3:
time: 97.3 us; the launch traced here: 95.3 us
  blocking collectives  84.5 us (87%)
  Pallas kernels  8.8 us (9%)
  local copies, waits for them, and re-layouts  1.94 us (2%)
    all_gather x5, blocking collectives, gather(): return lax.all_gather(x, 'space', axis_index_groups=groups)  39.9 us
    all_to_all x1, blocking collectives, shards(): lax.all_to_all(sent, 'energy', split_axis=0, concat_axis=0, tiled=True)  27.7 us
    all_to_all x1, blocking collectives, shards(): lax.all_to_all(result, 'energy', split_axis=0, concat_axis=0, tiled=True)  17 us
    pallas_call x1, Pallas kernels, scan_blocks(): call(lambda *refs: final_kernel(3, *refs), shape(TILE, 4, 2 * PACKED), [V...  2.23 us
    pallas_call x1, Pallas kernels, scan_blocks(): call(local_kernel, [shape(2, 2, n, n), shape(MAP, 2 * TILE)], [HB] * 2, s...  1.97 us

profile of v3, /device:TPU:14, one launch (start us, length us, event | category | flops | bytes accessed | tf_op | source)
XLA Modules:
  0.0 95.3 jit_solution(16701759583281752758)
XLA Ops:
  0.0 0.0 copy-start
  0.0 1.0 %copy-done = bf16[1,2,2,192,192]{4,3,2,1,0:T(8,128)(2,1)S(1)} copy-done((bf16[1,2,2,192,192]{4,3,2,1,0:T(8,128)(2,1)S(1)}, bf16[1,2,2,192,192]{4,3,2,1,0:T(8,128)(2,1)}, u32[]{:S(2)}) %copy-start) | copy-done | bytes 294936
  1.0 0.0 copy-start.3
  1.0 0.9 copy-done.3
  1.9 2.0 %shard_map.55 = (bf16[2,2,192,192]{3,2,1,0:T(8,128)(2,1)S(1)}, bf16[896,128]{1,0:T(8,128)(2,1)S(1)}) custom-call(bf16[2,2,192,192]{3,2,1,0:T(8,128)(2,1)S(1)} %bitcast.12, bf16[2,192,192]{2,1,0:T(8,128)(2,1)S(1)} %copy-done.3), custom_call_target="tpu_custom_call" | custom-call | tf_op jit(solution)/shard_map/pallas_call | solution.py:321
  3.9 2.1 %all-gather = bf16[1792,128]{1,0:T(8,128)(2,1)S(1)} all-gather(bf16[896,128]{1,0:T(8,128)(2,1)S(1)} %get-tuple-element.15), channel_id=2, replica_groups={{0,1},{2,3},{4,5},{6,7},{8,9},{10,11},{12,13},{14,15},{16,17},{18,19},{..., dimensions={0}, use_global_device_ids=true | all-gather | bytes 688128 | tf_op jit(solution)/shard_map/all_gather | solution.py:334
  6.0 1.1 %shard_map.56 = bf16[896,128]{1,0:T(8,128)(2,1)S(1)} custom-call(bf16[2,896,128]{2,1,0:T(8,128)(2,1)S(1)} %bitcast.8), custom_call_target="tpu_custom_call" | custom-call | tf_op jit(solution)/shard_map/pallas_call | solution.py:337
  7.2 0.0 copy-start.2
  7.2 8.4 %all-gather.1 = bf16[1792,128]{1,0:T(8,128)(2,1)S(1)} all-gather(bf16[896,128]{1,0:T(8,128)(2,1)S(1)} %shard_map.56), channel_id=3, replica_groups={{0,2},{1,3},{4,6},{5,7},{8,10},{9,11},{12,14},{13,15},{16,18},{17,19},{..., dimensions={0}, use_global_device_ids=true | all-gather | bytes 688128 | tf_op jit(solution)/shard_map/all_gather | solution.py:334
  15.6 0.0 copy-done.2
  15.6 1.3 %shard_map.57 = (bf16[2,2,192,192]{3,2,1,0:T(8,128)(2,1)S(1)}, bf16[64,640]{1,0:T(8,128)(2,1)S(1)}, bf16[64,640]{1,0:T(8,128)(2,1)S(1)}, bf16[2,64,640]{2,1,0:T(8,128)(2,1)S(1)}) custom-call(bf16[2,896,128]{2,1,0:T(8,128)(2,1)S(1)} %bitcast.10, bf16[2,2,192,192]{3,2,1,0:T(8,128)(2,1)S(1)} %bitcast.17), custom_call_target="tpu_custom_call" | custom-call | tf_op jit(solution)/shard_map/pallas_call | solution.py:339
  17.0 7.2 %all-gather.2 = bf16[128,640]{1,0:T(8,128)(2,1)S(1)} all-gather(bf16[64,640]{1,0:T(8,128)(2,1)S(1)} %get-tuple-element.16.refs_2_), channel_id=4, replica_groups={{0,4},{1,5},{2,6},{3,7},{8,12},{9,13},{10,14},{11,15},{16,20},{17,21},{..., dimensions={0}, use_global_device_ids=true | all-gather | bytes 245760 | tf_op jit(solution)/shard_map/all_gather | solution.py:334
  24.2 5.1 %all-gather.3 = bf16[128,640]{1,0:T(8,128)(2,1)S(1)} all-gather(bf16[64,640]{1,0:T(8,128)(2,1)S(1)} %get-tuple-element.19.refs_2_), channel_id=5, replica_groups={{0,2},{1,3},{4,8},{5,9},{6,10},{7,11},{12,14},{13,15},{16,18},{17,19},{..., dimensions={0}, use_global_device_ids=true | all-gather | bytes 245760 | tf_op jit(solution)/shard_map/all_gather | solution.py:334
  29.3 0.0 copy-start.1
  29.3 17.0 %all-gather.4 = bf16[128,640]{1,0:T(8,128)(2,1)S(1)} all-gather(bf16[64,640]{1,0:T(8,128)(2,1)S(1)} %get-tuple-element.21), channel_id=6, replica_groups={{0,4},{1,5},{2,6},{3,7},{8,12},{9,13},{10,14},{11,15},{16,20},{17,21},{..., dimensions={0}, use_global_device_ids=true | all-gather | bytes 245760 | tf_op jit(solution)/shard_map/all_gather | solution.py:334
  46.3 0.0 copy-done.1
  46.3 2.2 %shard_map.60 = bf16[64,4,640]{2,1,0:T(4,128)(2,1)S(1)} custom-call(bf16[2,64,640]{2,1,0:T(8,128)(2,1)S(1)} %bitcast.14, bf16[64,640]{1,0:T(8,128)(2,1)S(1)} %get-tuple-element.22.refs_1_, bf16[2,896,128]{2,1,0:T(8,128)(2,1)S(1)} %bitcast.11, bf16[2,896,128]{2,1,0:T(8,128)(2,1)S(1)} %bitcast.9, bf16[2,2,192,192]{3,2,1,0:T(8,128)(2,1)S(1)} %get-tuple-element.23.refs_4_, ...), custom_call_target="tpu_custom_call" | custom-call | tf_op jit(solution)/shard_map/pallas_call | solution.py:356
  48.6 0.0 copy-start.4
  48.6 0.0 copy-start.5
  48.6 27.7 %all_to_all.10.values = bf16[64,4,640]{2,1,0:T(4,128)(2,1)S(1)} all-to-all(bf16[64,4,640]{2,1,0:T(4,128)(2,1)S(1)} %shard_map.60), channel_id=1, replica_groups=mesh['energy'=64,'space'=16] {'energy'}, dimensions={0} | all-to-all | bytes 655360 | tf_op jit(solution)/shard_map/all_to_all | solution.py:369
  76.2 0.0 copy-done.4
  76.2 0.0 copy-done.5
  76.2 0.8 shard_map.61
  77.1 17.0 %all_to_all.11.packed = bf16[64,2,640]{2,1,0:T(2,128)(2,1)S(1)} all-to-all(bf16[64,2,640]{2,1,0:T(2,128)(2,1)S(1)} %shard_map.61), channel_id=1, replica_groups=mesh['energy'=64,'space'=16] {'energy'}, dimensions={0} | all-to-all | bytes 327680 | tf_op jit(solution)/shard_map/all_to_all | solution.py:374
  94.1 1.3 %shard_map.62 = bf16[2,2,192,192]{3,2,1,0:T(8,128)(2,1)} custom-call(bf16[64,2,640]{2,1,0:T(2,128)(2,1)S(1)} %all_to_all.11.packed), custom_call_target="tpu_custom_call" | custom-call | tf_op jit(solution)/shard_map/pallas_call | solution.py:375
  (2 shorter events, 0.0 us)
Async XLA Ops:
  0.0 1.0 %copy-start = (bf16[1,2,2,192,192]{4,3,2,1,0:T(8,128)(2,1)S(1)}, bf16[1,2,2,192,192]{4,3,2,1,0:T(8,128)(2,1)}, u32[]{:S(2)}) copy-start(bf16[1,2,2,192,192]{4,3,2,1,0:T(8,128)(2,1)} %param.5) | copy-start | bytes 884740
  1.0 0.9 copy-start.3
  7.2 8.4 %copy-start.2 = (bf16[1,2,2,192,192]{4,3,2,1,0:T(8,128)(2,1)S(1)}, bf16[1,2,2,192,192]{4,3,2,1,0:T(8,128)(2,1)}, u32[]{:S(2)}) copy-start(bf16[1,2,2,192,192]{4,3,2,1,0:T(8,128)(2,1)} %param.7) | copy-start | bytes 884740
  29.3 17.0 %copy-start.1 = (bf16[1,2,2,192,192]{4,3,2,1,0:T(8,128)(2,1)S(1)}, bf16[1,2,2,192,192]{4,3,2,1,0:T(8,128)(2,1)}, u32[]{:S(2)}) copy-start(bf16[1,2,2,192,192]{4,3,2,1,0:T(8,128)(2,1)} %param.5) | copy-start | bytes 884740
  48.6 27.7 %copy-start.4 = (bf16[128,256]{1,0:T(8,128)(2,1)S(1)}, bf16[128,256]{1,0:T(8,128)(2,1)}, u32[]{:S(2)}) copy-start(bf16[128,256]{1,0:T(8,128)(2,1)} %constant.5.clone.inverse) | copy-start | bytes 196612
  48.6 27.7 %copy-start.5 = (bf16[128,256]{1,0:T(8,128)(2,1)S(1)}, bf16[128,256]{1,0:T(8,128)(2,1)}, u32[]{:S(2)}) copy-start(bf16[128,256]{1,0:T(8,128)(2,1)} %constant.4.clone.forward) | copy-start | bytes 196612

commit v4 on v3

--- a/solution.py
+++ b/solution.py
@@ -14,6 +14,7 @@
 PACKED = 5 * TILE
 MAP = 14 * TILE
 VMEM_GRANT = 16 * 2**20
+FIRST_GRANT = 62 * 2**20
 
 VM = pl.BlockSpec(memory_space=pltpu.VMEM)
 HB = pl.BlockSpec(memory_space=pltpu.HBM)
@@ -108,14 +109,22 @@
     return unpack(parts[0], parts[1], parts[4]), unpack(parts[2], parts[3], half_turn(parts[4]))
 
 
+def store_slabs(ref, start, packed):
+    for k in range(5):
+        ref[start + k * TILE : start + (k + 1) * TILE] = packed[:, 2 * k * TILE : 2 * (k + 1) * TILE]
+
+
+def load_slabs(ref, start):
+    slabs = [ref[start + k * TILE : start + (k + 1) * TILE] for k in range(5)]
+    return jnp.concatenate(slabs, axis=1)
+
+
 def store_map(ref, a, c):
     n, w = 3 * TILE, 2 * TILE
     ref[:n] = a[0][:, :w]
     ref[n : 2 * n] = a[1][:, :w]
     ref[2 * n : 3 * n] = jnp.concatenate([a[0][:, w:], a[1][:, w:]], axis=1)
-    packed = pack_pair(c).astype(BF16)
-    for k in range(5):
-        ref[3 * n + k * TILE : 3 * n + (k + 1) * TILE] = packed[:, k * w : (k + 1) * w]
+    store_slabs(ref, 3 * n, pack_pair(c).astype(BF16))
 
 
 def load_map(ref):
@@ -125,8 +134,7 @@
         jnp.concatenate([ref[:n], rest[:, :TILE]], axis=1),
         jnp.concatenate([ref[n : 2 * n], rest[:, TILE:]], axis=1),
     )
-    packed = [ref[3 * n + k * TILE : 3 * n + (k + 1) * TILE] for k in range(5)]
-    return a, unpack_pair(jnp.concatenate(packed, axis=1))
+    return a, unpack_pair(load_slabs(ref, 3 * n))
 
 
 def load(ref, *at):
@@ -138,18 +146,23 @@
     ref[(*at, 1)] = pair[1]
 
 
-def local_kernel(green, coupling, transfer, aggregate, green_in, coupling_in, arrived):
+def local_kernel(
+    green, coupling, screened, transfer, aggregate, green_in, coupling_in, screened_in, arrived
+):
     copies = [
-        (
+        [
             pltpu.make_async_copy(coupling.at[b], coupling_in.at[b], arrived.at[b, 0]),
             pltpu.make_async_copy(green.at[b, 0], green_in.at[b, 0], arrived.at[b, 1]),
             pltpu.make_async_copy(green.at[b, 1], green_in.at[b, 1], arrived.at[b, 2]),
-        )
+        ]
         for b in range(2)
     ]
-    for block in copies:
-        for copy in block:
-            copy.start()
+    later = [
+        pltpu.make_async_copy(screened.at[b], screened_in.at[b], arrived.at[b, 3])
+        for b in range(2)
+    ]
+    for copy in copies[0] + copies[1] + later:
+        copy.start()
     maps = []
     for b in range(2):
         for copy in copies[b]:
@@ -161,6 +174,9 @@
         maps.append((t, g))
     (t0, g0), (t1, g1) = maps
     store_map(aggregate, rounded(complex_product(t1, t0, dot_nn)), sandwich(g0, t1, g1))
+    for b in range(2):
+        later[b].wait()
+        store_slabs(aggregate, MAP + b * PACKED, pack_pair(load(screened_in, b)).astype(BF16))
 
 
 def joined(maps):
@@ -172,14 +188,12 @@
     store_map(out, *joined(maps))
 
 
-def pair_kernel(maps, screened, out, end, prefix, screen):
+def pair_kernel(maps, out, end, prefix):
     prefix[...] = jnp.zeros(prefix.shape, BF16)
     a, c = joined(maps)
     store(out, a, 0)
     store(out, c, 1)
     end[...] = pack_pair(c).astype(BF16)
-    for b in range(2):
-        screen[b] = pack_pair(load(screened, b)).astype(BF16)
 
 
 def hop_kernel(hop, received, pair_map, end_in, prefix_in, end, prefix):
@@ -201,23 +215,42 @@
     return jnp.swapaxes(jnp.stack([p.astype(F32) for p in parts], axis=0), 0, 1).astype(BF16)
 
 
-def final_kernel(hop, received, prefix_in, chips, cores, transfer, green, screen, sent, state):
+def entry_kernel(hop, received, prefix, chips, entry, unused):
     index = lax.axis_index("space")
     mine = index // 4 == hop
-
-    @pl.when(mine)
-    def _():
-        store(state, unpack_pair(received[0]))
-
-    @pl.when(jnp.logical_not(mine))
-    def _():
-        store(state, unpack_pair(prefix_in[...]))
-
-    @pl.when(index // 2 % 2 == 1)
-    def _():
-        store(state, sandwich(load(state), *load_map(chips.at[0])))
-
-    @pl.when(index % 2 == 1)
+    before = jnp.where(mine, received[0], prefix[...])
+    odd = index // 2 % 2 == 1
+    unused[...] = jnp.zeros(unused.shape, BF16)
+    entry[TILE:] = jnp.zeros((TILE, 2 * PACKED), BF16)
+
+    @pl.when(odd)
+    def _():
+        c = sandwich(unpack_pair(before), *load_map(chips.at[0]))
+        entry[:TILE] = pack_pair(c).astype(BF16)
+
+    @pl.when(jnp.logical_not(odd))
+    def _():
+        entry[:TILE] = before
+
+
+def screen_kernel(cores, sent):
+    sent[...] = rows_first(
+        [load_slabs(cores.at[core], MAP + b * PACKED) for core in range(2) for b in range(2)]
+    )
+
+
+def regroup_kernel(values, theirs, mine):
+    x = jnp.swapaxes(values[...].astype(F32), 0, 1).astype(BF16)
+    points = values.shape[0]
+    for b in range(2):
+        mine[b] = x[b]
+        theirs[b * points : (b + 1) * points] = x[2 + b]
+
+
+def final_kernel(shared, cores, transfer, green, sent, state):
+    store(state, unpack_pair(shared[1, :TILE]))
+
+    @pl.when(lax.axis_index("space") % 2 == 1)
     def _():
         store(state, sandwich(load(state), *load_map(cores.at[0])))
 
@@ -226,7 +259,7 @@
     for b in range(2):
         carried = sandwich(carried, load(transfer, b), load(green, b))
         parts.append(pack_pair(carried))
-    sent[...] = rows_first(parts + [screen[0], screen[1]])
+    sent[...] = rows_first(parts)
 
 
 def split(table):
@@ -244,10 +277,22 @@
     return np.concatenate(split(forward), axis=1), np.concatenate(split(inverse), axis=1)
 
 
-def convolve_kernel(forward, inverse, values, out):
+def convolve_kernel(forward, inverse, values, shared, mine, out, screen):
     points, _, lanes = values.shape
     part = 4 * TILE
-    x = jnp.swapaxes(values[...].astype(F32), 0, 1)
+    even = lax.axis_index("space") % 2 == 0
+
+    @pl.when(even)
+    def _():
+        screen[...] = mine[...]
+
+    @pl.when(jnp.logical_not(even))
+    def _():
+        for b in range(2):
+            screen[b] = shared[0, b * points : (b + 1) * points]
+
+    g = jnp.swapaxes(values[...].astype(F32), 0, 1)
+    x = [g[0], g[1], screen[0].astype(F32), screen[1].astype(F32)]
     _, col = place_of((points, 2 * TILE))
     left = col < TILE
 
@@ -256,9 +301,9 @@
 
     re, im = [], []
     for k in (0, 2):
-        last_re, last_im = mixed(x[k, :, 2 * part :], x[k + 1, :, 2 * part :])
-        re += [x[k, :, :part], x[k + 1, :, :part], last_re]
-        im += [x[k, :, part : 2 * part], x[k + 1, :, part : 2 * part], last_im]
+        last_re, last_im = mixed(x[k][:, 2 * part :], x[k + 1][:, 2 * part :])
+        re += [x[k][:, :part], x[k + 1][:, :part], last_re]
+        im += [x[k][:, part : 2 * part], x[k + 1][:, part : 2 * part], last_im]
     re = jnp.concatenate(re, axis=1).astype(BF16)
     im = jnp.concatenate(im, axis=1).astype(BF16)
     spectra = dot_nn(forward[...], jnp.concatenate([re, im, re, im], axis=0))
@@ -295,7 +340,7 @@
         copy.wait()
 
 
-def call(kernel, out_shapes, specs, scratch=(), interpret=False, out_spec=VM):
+def call(kernel, out_shapes, specs, scratch=(), interpret=False, out_spec=VM, grant=VMEM_GRANT):
     many = isinstance(out_shapes, (list, tuple))
     return pl.pallas_call(
         kernel,
@@ -303,7 +348,7 @@
         in_specs=specs,
         out_specs=[out_spec] * len(out_shapes) if many else out_spec,
         scratch_shapes=scratch,
-        compiler_params=pltpu.CompilerParams(vmem_limit_bytes=VMEM_GRANT),
+        compiler_params=pltpu.CompilerParams(vmem_limit_bytes=grant),
         interpret=interpret,
     )
 
@@ -316,69 +361,92 @@
     return [[2 * low + core, 2 * high + core] for low, high in pairs for core in range(2)]
 
 
-def scan_blocks(green, coupling, screened, interpret=False):
+def scan_blocks(green, coupling, screened, exchange, interpret=False):
     n = green.shape[-1]
     transfer, aggregate = call(
         local_kernel,
-        [shape(2, 2, n, n), shape(MAP, 2 * TILE)],
-        [HB] * 2,
+        [shape(2, 2, n, n), shape(MAP + 2 * PACKED, 2 * TILE)],
+        [HB] * 3,
         scratch=[
             pltpu.VMEM((2, 2, n, n), BF16),
             pltpu.VMEM((2, n, n), BF16),
-            pltpu.SemaphoreType.DMA((2, 3)),
+            pltpu.VMEM((2, 2, n, n), BF16),
+            pltpu.SemaphoreType.DMA((2, 4)),
         ],
         interpret=interpret,
-    )(green, coupling)
+        grant=FIRST_GRANT,
+    )(green, coupling, screened)
 
     def gather(x, groups):
         return lax.all_gather(x, "space", axis_index_groups=groups)
 
-    cores = gather(aggregate, [[2 * c, 2 * c + 1] for c in range(8)])
-    chip = call(compose_kernel, shape(MAP, 2 * TILE), [VM], interpret=interpret)(cores)
-    chips = gather(chip, chip_groups([(0, 1), (2, 3), (4, 5), (6, 7)]))
-    pair_map, end, prefix, screen = call(
-        pair_kernel,
-        [shape(2, 2, n, n)] + [shape(TILE, 2 * PACKED)] * 2 + [shape(2, TILE, 2 * PACKED)],
-        [VM] * 2,
-        interpret=interpret,
-    )(chips, screened)
+    both = [[2 * c, 2 * c + 1] for c in range(8)]
     outer = chip_groups([(0, 2), (1, 3), (4, 6), (5, 7)])
     inner = chip_groups([(0, 1), (2, 4), (3, 5), (6, 7)])
-    for hop in (1, 2):
-        received = gather(end, outer if hop % 2 else inner)
-        end, prefix = call(
-            lambda *refs, hop=hop: hop_kernel(hop, *refs),
-            [shape(TILE, 2 * PACKED)] * 2,
-            [VM] * 4,
-            interpret=interpret,
-        )(received, pair_map, end, prefix)
-    received = gather(end, outer)
-    return call(
-        lambda *refs: final_kernel(3, *refs),
-        shape(TILE, 4, 2 * PACKED),
-        [VM] * 7,
+    packed = shape(TILE, 2 * PACKED)
+    points = TILE
+    leaving = [shape(2 * points, 2 * PACKED), shape(2, points, 2 * PACKED)]
+
+    def chain(cores):
+        chip = call(compose_kernel, shape(MAP, 2 * TILE), [VM], interpret=interpret)(cores)
+        chips = gather(chip, chip_groups([(0, 1), (2, 3), (4, 5), (6, 7)]))
+        pair_map, end, prefix = call(
+            pair_kernel, [shape(2, 2, n, n), packed, packed], [VM], interpret=interpret
+        )(chips)
+        for hop in (1, 2):
+            received = gather(end, outer if hop % 2 else inner)
+            end, prefix = call(
+                lambda *refs, hop=hop: hop_kernel(hop, *refs),
+                [packed] * 2,
+                [VM] * 4,
+                interpret=interpret,
+            )(received, pair_map, end, prefix)
+        received = gather(end, outer)
+        return tuple(
+            call(lambda *refs: entry_kernel(3, *refs), leaving, [VM] * 3, interpret=interpret)(
+                received, prefix, chips
+            )
+        )
+
+    def exchange_screen(cores):
+        sent = call(screen_kernel, shape(TILE, 4, 2 * PACKED), [VM], interpret=interpret)(cores)
+        return tuple(call(regroup_kernel, leaving, [VM], interpret=interpret)(exchange(sent)))
+
+    cores = gather(aggregate, both)
+    leave, mine = lax.cond(lax.axis_index("space") % 2 == 1, chain, exchange_screen, cores)
+    shared = gather(leave, both)
+    sent = call(
+        final_kernel,
+        shape(TILE, 2, 2 * PACKED),
+        [VM] * 4,
         scratch=[pltpu.VMEM((2, n, n), BF16)],
         interpret=interpret,
-    )(received, prefix, chips, cores, transfer, green, screen)
+    )(shared, cores, transfer, green)
+    return sent, shared, mine
 
 
 def shards(iso_green, coupling, screened):
     points = lax.axis_size("energy")
     n = iso_green.shape[-1]
-    sent = scan_blocks(iso_green[0], coupling, screened[0])
-    values = lax.all_to_all(sent, "energy", split_axis=0, concat_axis=0, tiled=True)
+
+    def exchange(x):
+        return lax.all_to_all(x, "energy", split_axis=0, concat_axis=0, tiled=True)
+
+    sent, shared, mine = scan_blocks(iso_green[0], coupling, screened[0], exchange)
     forward, inverse = tables(points)
-    result = call(convolve_kernel, shape(points, 2, 2 * PACKED), [VM] * 3)(
-        jnp.asarray(forward), jnp.asarray(inverse), values
-    )
-    returned = lax.all_to_all(result, "energy", split_axis=0, concat_axis=0, tiled=True)
+    result = call(
+        convolve_kernel,
+        shape(points, 2, 2 * PACKED),
+        [VM] * 5,
+        scratch=[pltpu.VMEM((2, points, 2 * PACKED), BF16)],
+    )(jnp.asarray(forward), jnp.asarray(inverse), exchange(sent), shared, mine)
     return call(
         unpack_kernel,
         shape(2, 2, n, n),
         [VM],
         scratch=[pltpu.VMEM((2, 2, n, n), BF16), pltpu.SemaphoreType.DMA((2,))],
         out_spec=HB,
-    )(returned)[None]
+    )(exchange(result))[None]
 
 
 def solution(mesh):

time: 97.3 us -> 93 us (0.956)
  local copies, waits for them, and re-layouts: 1.94 us -> 0.02 us
  Pallas kernels: 8.8 us -> 7.51 us
    all_gather x5 -> x2, blocking collectives: 39.9 us -> 4.75 us  [gather(): return lax.all_gather(x, 'space', axis_index_groups=groups)]
    all_to_all x2 -> x3, blocking collectives: 44.6 us -> 79.2 us  [exchange(): return lax.all_to_all(x, 'energy', split_axis=0, concat_axis=0, tiled=True)]
    unnamed x12 -> x8, local copies, waits for them, and re-layouts: 1.94 us -> 0.02 us
    pallas_call x7 -> x5, Pallas kernels: 7.52 us -> 6.23 us  [the longest x1 3.39 us: scan_blocks(): call(local_kernel, [shape(2, 2, n, n), shape(MAP + 2 * PACKED, 2 * TILE)]...]
where the time goes in v4:
time: 93 us; the launch traced here: 91.5 us
  blocking collectives  83.9 us (90%)
  Pallas kernels  7.51 us (8%)
    all_to_all x3, blocking collectives, exchange(): return lax.all_to_all(x, 'energy', split_axis=0, concat_axis=0, tiled=True)  79.2 us
    all_gather x2, blocking collectives, gather(): return lax.all_gather(x, 'space', axis_index_groups=groups)  4.75 us
    pallas_call x1, Pallas kernels, scan_blocks(): call(local_kernel, [shape(2, 2, n, n), shape(MAP + 2 * PACKED, 2 * TILE)]...  3.39 us

profile of v4, /device:TPU:14, one launch (start us, length us, event | category | flops | bytes accessed | tf_op | source)
XLA Modules:
  0.0 91.5 jit_solution(13850568104346990881)
XLA Ops:
  0.0 3.4 %shard_map.55 = (bf16[2,2,192,192]{3,2,1,0:T(8,128)(2,1)}, bf16[1536,128]{1,0:T(8,128)(2,1)}) custom-call(bf16[2,2,192,192]{3,2,1,0:T(8,128)(2,1)} %bitcast.13, bf16[2,192,192]{2,1,0:T(8,128)(2,1)} %coupling.1, bf16[2,2,192,192]{3,2,1,0:T(8,128)(2,1)} %bitcast.21), custom_call_target="tpu_custom_call" | custom-call | tf_op jit(solution)/shard_map/pallas_call | solution.py:366
  3.4 2.6 %all-gather.4 = bf16[3072,128]{1,0:T(8,128)(2,1)S(1)} all-gather(bf16[1536,128]{1,0:T(8,128)(2,1)} %get-tuple-element.18), channel_id=6, replica_groups={{0,1},{2,3},{4,5},{6,7},{8,9},{10,11},{12,13},{14,15},{16,17},{18,19},{..., dimensions={0}, use_global_device_ids=true | all-gather | bytes 1179648 | tf_op jit(solution)/shard_map/all_gather | solution.py:381
  6.0 0.0 copy-start.1
  6.0 37.6 %conditional.1 = ((bf16[128,640]{1,0:T(8,128)(2,1)S(1)}, bf16[2,64,640]{2,1,0:T(8,128)(2,1)S(1)})) conditional(s32[]{:T(128)} %convert_element_type.3, bf16[2,1536,128]{2,1,0:T(8,128)(2,1)S(1)} %bitcast.18, bf16[2,1536,128]{2,1,0:T(8,128)(2,1)S(1)} %bitcast.19), branch_computations={%region_0.1_spmd, %region_1.2_spmd} | conditional | bytes 1425416 | solution.py:416
  6.0 0.2 branch_0_fun.2
  6.2 37.2 %all_to_all.14.values = bf16[64,4,640]{2,1,0:T(4,128)(2,1)S(1)} all-to-all(bf16[64,4,640]{2,1,0:T(4,128)(2,1)S(1)} %branch_0_fun.2), channel_id=1, replica_groups=mesh['energy'=64,'space'=16] {'energy'}, dimensions={0} | all-to-all | bytes 655360 | tf_op jit(solution)/shard_map/cond/branch_0_fun/all_to_all | solution.py:433
  43.4 0.2 branch_0_fun.3
  43.6 0.0 copy-start
  43.6 2.2 %all-gather.5 = bf16[256,640]{1,0:T(8,128)(2,1)S(1)} all-gather(bf16[128,640]{1,0:T(8,128)(2,1)S(1)} %get-tuple-element.19), channel_id=7, replica_groups={{0,1},{2,3},{4,5},{6,7},{8,9},{10,11},{12,13},{14,15},{16,17},{18,19},{..., dimensions={0}, use_global_device_ids=true | all-gather | bytes 491520 | tf_op jit(solution)/shard_map/all_gather | solution.py:381
  45.8 0.0 copy-done.1
  45.8 0.0 copy-done
  45.8 1.7 %shard_map.56 = bf16[64,2,640]{2,1,0:T(2,128)(2,1)S(1)} custom-call(bf16[2,128,640]{2,1,0:T(8,128)(2,1)S(1)} %bitcast.11, bf16[2,1536,128]{2,1,0:T(8,128)(2,1)S(1)} %bitcast.20, bf16[2,2,192,192]{3,2,1,0:T(8,128)(2,1)S(1)} %copy-done.1, bf16[2,2,192,192]{3,2,1,0:T(8,128)(2,1)S(1)} %bitcast.14), custom_call_target="tpu_custom_call" | custom-call | tf_op jit(solution)/shard_map/pallas_call | solution.py:418
  47.5 0.0 copy-start.2
  47.5 0.0 copy-start.3
  47.5 25.1 %all_to_all.15.values = bf16[64,2,640]{2,1,0:T(2,128)(2,1)S(1)} all-to-all(bf16[64,2,640]{2,1,0:T(2,128)(2,1)S(1)} %shard_map.56), channel_id=1, replica_groups=mesh['energy'=64,'space'=16] {'energy'}, dimensions={0} | all-to-all | bytes 327680 | tf_op jit(solution)/shard_map/all_to_all | solution.py:433
  72.6 0.0 copy-done.2
  72.6 0.0 copy-done.3
  72.6 0.8 shard_map.57
  73.4 16.8 %all_to_all.16.packed = bf16[64,2,640]{2,1,0:T(2,128)(2,1)S(1)} all-to-all(bf16[64,2,640]{2,1,0:T(2,128)(2,1)S(1)} %shard_map.57), channel_id=1, replica_groups=mesh['energy'=64,'space'=16] {'energy'}, dimensions={0} | all-to-all | bytes 327680 | tf_op jit(solution)/shard_map/all_to_all | solution.py:433
  90.3 1.3 %shard_map.58 = bf16[2,2,192,192]{3,2,1,0:T(8,128)(2,1)} custom-call(bf16[64,2,640]{2,1,0:T(2,128)(2,1)S(1)} %all_to_all.16.packed), custom_call_target="tpu_custom_call" | custom-call | tf_op jit(solution)/shard_map/pallas_call | solution.py:443
Async XLA Ops:
  6.0 39.8 %copy-start.1 = (bf16[2,2,192,192]{3,2,1,0:T(8,128)(2,1)S(1)}, bf16[2,2,192,192]{3,2,1,0:T(8,128)(2,1)}, u32[]{:S(2)}) copy-start(bf16[2,2,192,192]{3,2,1,0:T(8,128)(2,1)} %get-tuple-element.20.transfer) | copy-start | bytes 884740
  43.6 2.2 %copy-start = (bf16[1,2,2,192,192]{4,3,2,1,0:T(8,128)(2,1)S(1)}, bf16[1,2,2,192,192]{4,3,2,1,0:T(8,128)(2,1)}, u32[]{:S(2)}) copy-start(bf16[1,2,2,192,192]{4,3,2,1,0:T(8,128)(2,1)} %param.7) | copy-start | bytes 884740
  47.5 25.1 %copy-start.2 = (bf16[128,256]{1,0:T(8,128)(2,1)S(1)}, bf16[128,256]{1,0:T(8,128)(2,1)}, u32[]{:S(2)}) copy-start(bf16[128,256]{1,0:T(8,128)(2,1)} %constant.23.clone.inverse) | copy-start | bytes 196612
  47.5 25.1 %copy-start.3 = (bf16[128,256]{1,0:T(8,128)(2,1)S(1)}, bf16[128,256]{1,0:T(8,128)(2,1)}, u32[]{:S(2)}) copy-start(bf16[128,256]{1,0:T(8,128)(2,1)} %constant.22.clone.forward) | copy-start | bytes 196612

commit v5 on v4

--- a/solution.py
+++ b/solution.py
@@ -14,7 +14,6 @@
 PACKED = 5 * TILE
 MAP = 14 * TILE
 VMEM_GRANT = 16 * 2**20
-FIRST_GRANT = 62 * 2**20
 
 VM = pl.BlockSpec(memory_space=pltpu.VMEM)
 HB = pl.BlockSpec(memory_space=pltpu.HBM)
@@ -56,6 +55,12 @@
 
 def widened(x):
     return jnp.concatenate([x, x], axis=1)
+
+
+def sandwich_packed(carried, factor, source):
+    middle = rounded(complex_product(carried, factor, dot_nt))
+    total = pack_pair(complex_product(factor, middle, dot_nn)) + source.astype(F32)
+    return total.astype(BF16)
 
 
 def pack(m):
@@ -119,12 +124,12 @@
     return jnp.concatenate(slabs, axis=1)
 
 
-def store_map(ref, a, c):
+def store_map(ref, a, packed):
     n, w = 3 * TILE, 2 * TILE
     ref[:n] = a[0][:, :w]
     ref[n : 2 * n] = a[1][:, :w]
     ref[2 * n : 3 * n] = jnp.concatenate([a[0][:, w:], a[1][:, w:]], axis=1)
-    store_slabs(ref, 3 * n, pack_pair(c).astype(BF16))
+    store_slabs(ref, 3 * n, packed)
 
 
 def load_map(ref):
@@ -134,7 +139,7 @@
         jnp.concatenate([ref[:n], rest[:, :TILE]], axis=1),
         jnp.concatenate([ref[n : 2 * n], rest[:, TILE:]], axis=1),
     )
-    return a, unpack_pair(load_slabs(ref, 3 * n))
+    return a, load_slabs(ref, 3 * n)
 
 
 def load(ref, *at):
@@ -170,10 +175,12 @@
         k = coupling_in[b]
         g = load(green_in, b)
         t = rounded((dot_nn(g[0], k), dot_nn(g[1], k)))
-        store(transfer, t, b)
+        if b == 0:
+            store(transfer, t)
         maps.append((t, g))
     (t0, g0), (t1, g1) = maps
-    store_map(aggregate, rounded(complex_product(t1, t0, dot_nn)), sandwich(g0, t1, g1))
+    c = pack_pair(sandwich(g0, t1, g1)).astype(BF16)
+    store_map(aggregate, rounded(complex_product(t1, t0, dot_nn)), c)
     for b in range(2):
         later[b].wait()
         store_slabs(aggregate, MAP + b * PACKED, pack_pair(load(screened_in, b)).astype(BF16))
@@ -181,7 +188,8 @@
 
 def joined(maps):
     (a_low, c_low), (a_high, c_high) = load_map(maps.at[0]), load_map(maps.at[1])
-    return rounded(complex_product(a_high, a_low, dot_nn)), sandwich(c_low, a_high, c_high)
+    a = rounded(complex_product(a_high, a_low, dot_nn))
+    return a, sandwich_packed(unpack_pair(c_low), a_high, c_high)
 
 
 def compose_kernel(maps, out):
@@ -191,19 +199,18 @@
 def pair_kernel(maps, out, end, prefix):
     prefix[...] = jnp.zeros(prefix.shape, BF16)
     a, c = joined(maps)
-    store(out, a, 0)
-    store(out, c, 1)
-    end[...] = pack_pair(c).astype(BF16)
-
-
-def hop_kernel(hop, received, pair_map, end_in, prefix_in, end, prefix):
+    store(out, a)
+    end[...] = c
+
+
+def hop_kernel(hop, received, pair_a, pair_c, end_in, prefix_in, end, prefix):
     mine = lax.axis_index("space") // 4 == hop
 
     @pl.when(mine)
     def _():
-        before = unpack_pair(received[0])
-        end[...] = pack_pair(sandwich(before, load(pair_map, 0), load(pair_map, 1))).astype(BF16)
-        prefix[...] = received[0]
+        before = received[0]
+        end[...] = sandwich_packed(unpack_pair(before), load(pair_a), pair_c[...])
+        prefix[...] = before
 
     @pl.when(jnp.logical_not(mine))
     def _():
@@ -225,15 +232,15 @@
 
     @pl.when(odd)
     def _():
-        c = sandwich(unpack_pair(before), *load_map(chips.at[0]))
-        entry[:TILE] = pack_pair(c).astype(BF16)
+        entry[:TILE] = sandwich_packed(unpack_pair(before), *load_map(chips.at[0]))
 
     @pl.when(jnp.logical_not(odd))
     def _():
         entry[:TILE] = before
 
 
-def screen_kernel(cores, sent):
+def screen_kernel(cores, sent, last_map):
+    last_map[...] = cores[0, :MAP]
     sent[...] = rows_first(
         [load_slabs(cores.at[core], MAP + b * PACKED) for core in range(2) for b in range(2)]
     )
@@ -247,19 +254,18 @@
         theirs[b * points : (b + 1) * points] = x[2 + b]
 
 
-def final_kernel(shared, cores, transfer, green, sent, state):
-    store(state, unpack_pair(shared[1, :TILE]))
+def final_kernel(shared, cores, last_map, transfer, green, sent, state):
+    entry = unpack_pair(shared[1, :TILE])
+    store(state, entry)
 
     @pl.when(lax.axis_index("space") % 2 == 1)
     def _():
-        store(state, sandwich(load(state), *load_map(cores.at[0])))
-
-    carried = load(state)
-    parts = []
-    for b in range(2):
-        carried = sandwich(carried, load(transfer, b), load(green, b))
-        parts.append(pack_pair(carried))
-    sent[...] = rows_first(parts)
+        a, c = load_map(cores.at[0])
+        store(state, sandwich(entry, a, unpack_pair(c)))
+
+    last = sandwich_packed(entry, *load_map(last_map))
+    first = sandwich(load(state), load(transfer), load(green, 0))
+    sent[...] = rows_first([pack_pair(first), last])
 
 
 def split(table):
@@ -340,7 +346,7 @@
         copy.wait()
 
 
-def call(kernel, out_shapes, specs, scratch=(), interpret=False, out_spec=VM, grant=VMEM_GRANT):
+def call(kernel, out_shapes, specs, scratch=(), interpret=False, out_spec=VM):
     many = isinstance(out_shapes, (list, tuple))
     return pl.pallas_call(
         kernel,
@@ -348,7 +354,7 @@
         in_specs=specs,
         out_specs=[out_spec] * len(out_shapes) if many else out_spec,
         scratch_shapes=scratch,
-        compiler_params=pltpu.CompilerParams(vmem_limit_bytes=grant),
+        compiler_params=pltpu.CompilerParams(vmem_limit_bytes=VMEM_GRANT),
         interpret=interpret,
     )
 
@@ -365,7 +371,7 @@
     n = green.shape[-1]
     transfer, aggregate = call(
         local_kernel,
-        [shape(2, 2, n, n), shape(MAP + 2 * PACKED, 2 * TILE)],
+        [shape(2, n, n), shape(MAP + 2 * PACKED, 2 * TILE)],
         [HB] * 3,
         scratch=[
             pltpu.VMEM((2, 2, n, n), BF16),
@@ -374,8 +380,7 @@
             pltpu.SemaphoreType.DMA((2, 4)),
         ],
         interpret=interpret,
-        grant=FIRST_GRANT,
-    )(green, coupling, screened)
+    )(*(pltpu.with_memory_space_constraint(x, pltpu.HBM) for x in (green, coupling, screened)))
 
     def gather(x, groups):
         return lax.all_gather(x, "space", axis_index_groups=groups)
@@ -390,38 +395,45 @@
     def chain(cores):
         chip = call(compose_kernel, shape(MAP, 2 * TILE), [VM], interpret=interpret)(cores)
         chips = gather(chip, chip_groups([(0, 1), (2, 3), (4, 5), (6, 7)]))
-        pair_map, end, prefix = call(
-            pair_kernel, [shape(2, 2, n, n), packed, packed], [VM], interpret=interpret
+        pair_a, end, prefix = call(
+            pair_kernel, [shape(2, n, n), packed, packed], [VM], interpret=interpret
         )(chips)
+        pair_c = end
         for hop in (1, 2):
             received = gather(end, outer if hop % 2 else inner)
             end, prefix = call(
                 lambda *refs, hop=hop: hop_kernel(hop, *refs),
                 [packed] * 2,
-                [VM] * 4,
+                [VM] * 5,
                 interpret=interpret,
-            )(received, pair_map, end, prefix)
+            )(received, pair_a, pair_c, end, prefix)
         received = gather(end, outer)
-        return tuple(
-            call(lambda *refs: entry_kernel(3, *refs), leaving, [VM] * 3, interpret=interpret)(
-                received, prefix, chips
-            )
-        )
+        leave, unused = call(
+            lambda *refs: entry_kernel(3, *refs), leaving, [VM] * 3, interpret=interpret
+        )(received, prefix, chips)
+        return leave, unused, chip
 
     def exchange_screen(cores):
-        sent = call(screen_kernel, shape(TILE, 4, 2 * PACKED), [VM], interpret=interpret)(cores)
-        return tuple(call(regroup_kernel, leaving, [VM], interpret=interpret)(exchange(sent)))
+        sent, last_map = call(
+            screen_kernel,
+            [shape(TILE, 4, 2 * PACKED), shape(MAP, 2 * TILE)],
+            [VM],
+            interpret=interpret,
+        )(cores)
+        leave, mine = call(regroup_kernel, leaving, [VM], interpret=interpret)(exchange(sent))
+        return leave, mine, last_map
 
     cores = gather(aggregate, both)
-    leave, mine = lax.cond(lax.axis_index("space") % 2 == 1, chain, exchange_screen, cores)
+    odd = lax.axis_index("space") % 2 == 1
+    leave, mine, last_map = lax.cond(odd, chain, exchange_screen, cores)
     shared = gather(leave, both)
     sent = call(
         final_kernel,
         shape(TILE, 2, 2 * PACKED),
-        [VM] * 4,
+        [VM] * 5,
         scratch=[pltpu.VMEM((2, n, n), BF16)],
         interpret=interpret,
-    )(shared, cores, transfer, green)
+    )(shared, cores, last_map, transfer, green)
     return sent, shared, mine
 
 

time: 93 us -> 92 us (0.989)
  no operation moved by 1% of the time
where the time goes in v5:
time: 92 us; the launch traced here: 90.5 us
  blocking collectives  83.7 us (91%)
  Pallas kernels  6.67 us (7%)
    all_to_all x3, blocking collectives, exchange(): return lax.all_to_all(x, 'energy', split_axis=0, concat_axis=0, tiled=True)  79.2 us
    all_gather x2, blocking collectives, gather(): return lax.all_gather(x, 'space', axis_index_groups=groups)  4.54 us
    pallas_call x1, Pallas kernels, scan_blocks(): call(local_kernel, [shape(2, n, n), shape(MAP + 2 * PACKED, 2 * TILE)], [...  2.61 us

profile of v5, /device:TPU:14, one launch (start us, length us, event | category | flops | bytes accessed | tf_op | source)
XLA Modules:
  0.0 90.5 jit_solution(6560825856951599164)
XLA Ops:
  0.0 2.6 %shard_map.55 = (bf16[2,192,192]{2,1,0:T(8,128)(2,1)S(1)}, bf16[1536,128]{1,0:T(8,128)(2,1)S(1)}) custom-call(bf16[2,2,192,192]{3,2,1,0:T(8,128)(2,1)} %bitcast.13, bf16[2,192,192]{2,1,0:T(8,128)(2,1)} %coupling.1, bf16[2,2,192,192]{3,2,1,0:T(8,128)(2,1)} %bitcast.21), custom_call_target="tpu_custom_call" | custom-call | tf_op jit(solution)/shard_map/pallas_call | solution.py:372
  2.6 2.4 %all-gather.4 = bf16[3072,128]{1,0:T(8,128)(2,1)S(1)} all-gather(bf16[1536,128]{1,0:T(8,128)(2,1)S(1)} %get-tuple-element.25), channel_id=6, replica_groups={{0,1},{2,3},{4,5},{6,7},{8,9},{10,11},{12,13},{14,15},{16,17},{18,19},{..., dimensions={0}, use_global_device_ids=true | all-gather | bytes 1179648 | tf_op jit(solution)/shard_map/all_gather | solution.py:386
  5.0 37.6 %conditional.1 = (bf16[128,640]{1,0:T(8,128)(2,1)S(1)}, bf16[2,64,640]{2,1,0:T(8,128)(2,1)S(1)}, bf16[896,128]{1,0:T(8,128)(2,1)S(1)}) conditional(s32[]{:T(128)} %convert_element_type.3, bf16[2,1536,128]{2,1,0:T(8,128)(2,1)S(1)} %bitcast.18, bf16[2,1536,128]{2,1,0:T(8,128)(2,1)S(1)} %bitcast.19), branch_computations={%region_0.1_spmd, %region_1.2_spmd} | conditional | bytes 3260496 | solution.py:428
  5.0 0.2 branch_0_fun.2
  5.2 37.2 %all_to_all.14.values = bf16[64,4,640]{2,1,0:T(4,128)(2,1)S(1)} all-to-all(bf16[64,4,640]{2,1,0:T(4,128)(2,1)S(1)} %get-tuple-element.7), channel_id=1, replica_groups=mesh['energy'=64,'space'=16] {'energy'}, dimensions={0} | all-to-all | bytes 655360 | tf_op jit(solution)/shard_map/cond/branch_0_fun/all_to_all | solution.py:445
  42.4 0.2 branch_0_fun.3
  42.6 0.0 copy-start
  42.6 2.2 %all-gather.5 = bf16[256,640]{1,0:T(8,128)(2,1)S(1)} all-gather(bf16[128,640]{1,0:T(8,128)(2,1)S(1)} %get-tuple-element.26), channel_id=7, replica_groups={{0,1},{2,3},{4,5},{6,7},{8,9},{10,11},{12,13},{14,15},{16,17},{18,19},{..., dimensions={0}, use_global_device_ids=true | all-gather | bytes 491520 | tf_op jit(solution)/shard_map/all_gather | solution.py:386
  44.8 0.0 copy-done
  44.8 1.6 %shard_map.56 = bf16[64,2,640]{2,1,0:T(2,128)(2,1)S(1)} custom-call(bf16[2,128,640]{2,1,0:T(8,128)(2,1)S(1)} %bitcast.11, bf16[2,1536,128]{2,1,0:T(8,128)(2,1)S(1)} %bitcast.20, bf16[896,128]{1,0:T(8,128)(2,1)S(1)} %get-tuple-element.27.last_map, bf16[2,192,192]{2,1,0:T(8,128)(2,1)S(1)} %get-tuple-element.28.transfer, bf16[2,2,192,192]{3,2,1,0:T(8,128)(2,1)S(1)} %bitcast.14), custom_call_target="tpu_custom_call" | custom-call | tf_op jit(solution)/shard_map/pallas_call | solution.py:430
  46.4 0.0 copy-start.1
  46.4 0.0 copy-start.2
  46.4 25.1 %all_to_all.15.values = bf16[64,2,640]{2,1,0:T(2,128)(2,1)S(1)} all-to-all(bf16[64,2,640]{2,1,0:T(2,128)(2,1)S(1)} %shard_map.56), channel_id=1, replica_groups=mesh['energy'=64,'space'=16] {'energy'}, dimensions={0} | all-to-all | bytes 327680 | tf_op jit(solution)/shard_map/all_to_all | solution.py:445
  71.6 0.0 copy-done.1
  71.6 0.0 copy-done.2
  71.6 0.8 shard_map.57
  72.4 16.8 %all_to_all.16.packed = bf16[64,2,640]{2,1,0:T(2,128)(2,1)S(1)} all-to-all(bf16[64,2,640]{2,1,0:T(2,128)(2,1)S(1)} %shard_map.57), channel_id=1, replica_groups=mesh['energy'=64,'space'=16] {'energy'}, dimensions={0} | all-to-all | bytes 327680 | tf_op jit(solution)/shard_map/all_to_all | solution.py:445
  89.2 1.3 %shard_map.58 = bf16[2,2,192,192]{3,2,1,0:T(8,128)(2,1)} custom-call(bf16[64,2,640]{2,1,0:T(2,128)(2,1)S(1)} %all_to_all.16.packed), custom_call_target="tpu_custom_call" | custom-call | tf_op jit(solution)/shard_map/pallas_call | solution.py:455
Async XLA Ops:
  42.6 2.2 %copy-start = (bf16[1,2,2,192,192]{4,3,2,1,0:T(8,128)(2,1)S(1)}, bf16[1,2,2,192,192]{4,3,2,1,0:T(8,128)(2,1)}, u32[]{:S(2)}) copy-start(bf16[1,2,2,192,192]{4,3,2,1,0:T(8,128)(2,1)} %param.7) | copy-start | bytes 884740
  46.4 25.2 %copy-start.1 = (bf16[128,256]{1,0:T(8,128)(2,1)S(1)}, bf16[128,256]{1,0:T(8,128)(2,1)}, u32[]{:S(2)}) copy-start(bf16[128,256]{1,0:T(8,128)(2,1)} %constant.23.clone.inverse) | copy-start | bytes 196612
  46.4 25.2 %copy-start.2 = (bf16[128,256]{1,0:T(8,128)(2,1)S(1)}, bf16[128,256]{1,0:T(8,128)(2,1)}, u32[]{:S(2)}) copy-start(bf16[128,256]{1,0:T(8,128)(2,1)} %constant.22.clone.forward) | copy-start | bytes 196612

commit v6 on v5

--- a/solution.py
+++ b/solution.py
@@ -186,55 +186,60 @@
         store_slabs(aggregate, MAP + b * PACKED, pack_pair(load(screened_in, b)).astype(BF16))
 
 
-def joined(maps):
-    (a_low, c_low), (a_high, c_high) = load_map(maps.at[0]), load_map(maps.at[1])
+def joined(low, high):
+    (a_low, c_low), (a_high, c_high) = load_map(low), load_map(high)
     a = rounded(complex_product(a_high, a_low, dot_nn))
     return a, sandwich_packed(unpack_pair(c_low), a_high, c_high)
 
 
 def compose_kernel(maps, out):
-    store_map(out, *joined(maps))
-
-
-def pair_kernel(maps, out, end, prefix):
-    prefix[...] = jnp.zeros(prefix.shape, BF16)
-    a, c = joined(maps)
-    store(out, a)
-    end[...] = c
-
-
-def hop_kernel(hop, received, pair_a, pair_c, end_in, prefix_in, end, prefix):
-    mine = lax.axis_index("space") // 4 == hop
-
-    @pl.when(mine)
-    def _():
-        before = received[0]
-        end[...] = sandwich_packed(unpack_pair(before), load(pair_a), pair_c[...])
-        prefix[...] = before
-
-    @pl.when(jnp.logical_not(mine))
-    def _():
-        end[...] = end_in[...]
-        prefix[...] = prefix_in[...]
+    store_map(out, *joined(maps.at[0], maps.at[1]))
+
+
+def middle_kernel(pairs, chips, end, before, onward):
+    index = lax.axis_index("space")
+    pair, odd = index // 4, index // 2 % 2 == 1
+    first = load_slabs(pairs.at[0], 9 * TILE)
+    before[...] = jnp.where(pair == 1, first, jnp.zeros_like(first))
+
+    @pl.when(pair < 2)
+    def _():
+        end[...] = sandwich_packed(unpack_pair(first), *load_map(pairs.at[1]))
+
+    @pl.when(pair >= 2)
+    def _():
+        end[...] = first
+
+    @pl.when(pair < 3)
+    def _():
+        onward[...] = chips[0]
+
+    @pl.when((pair == 3) & jnp.logical_not(odd))
+    def _():
+        onward[...] = pairs[0]
+
+    @pl.when((pair == 3) & odd)
+    def _():
+        store_map(onward, *joined(pairs.at[0], chips.at[0]))
 
 
 def rows_first(parts):
-    return jnp.swapaxes(jnp.stack([p.astype(F32) for p in parts], axis=0), 0, 1).astype(BF16)
-
-
-def entry_kernel(hop, received, prefix, chips, entry, unused):
+    return jnp.swapaxes(jnp.stack([p.astype(BF16) for p in parts], axis=0), 0, 1)
+
+
+def entry_kernel(received, before_in, onward, entry, unused):
     index = lax.axis_index("space")
-    mine = index // 4 == hop
-    before = jnp.where(mine, received[0], prefix[...])
-    odd = index // 2 % 2 == 1
+    pair, odd = index // 4, index // 2 % 2 == 1
+    before = jnp.where(pair < 2, before_in[...], received[0])
     unused[...] = jnp.zeros(unused.shape, BF16)
     entry[TILE:] = jnp.zeros((TILE, 2 * PACKED), BF16)
-
-    @pl.when(odd)
-    def _():
-        entry[:TILE] = sandwich_packed(unpack_pair(before), *load_map(chips.at[0]))
-
-    @pl.when(jnp.logical_not(odd))
+    moved = odd | (pair == 3)
+
+    @pl.when(moved)
+    def _():
+        entry[:TILE] = sandwich_packed(unpack_pair(before), *load_map(onward))
+
+    @pl.when(jnp.logical_not(moved))
     def _():
         entry[:TILE] = before
 
@@ -247,25 +252,31 @@
 
 
 def regroup_kernel(values, theirs, mine):
-    x = jnp.swapaxes(values[...].astype(F32), 0, 1).astype(BF16)
+    x = jnp.swapaxes(values[...], 0, 1)
     points = values.shape[0]
     for b in range(2):
         mine[b] = x[b]
         theirs[b * points : (b + 1) * points] = x[2 + b]
 
 
-def final_kernel(shared, cores, last_map, transfer, green, sent, state):
-    entry = unpack_pair(shared[1, :TILE])
-    store(state, entry)
-
-    @pl.when(lax.axis_index("space") % 2 == 1)
-    def _():
+def final_kernel(shared, cores, last_map, transfer, green, sent):
+    odd = lax.axis_index("space") % 2 == 1
+
+    def finish(entry, before):
+        first = sandwich(before, load(transfer), load(green, 0))
+        last = sandwich_packed(entry, *load_map(last_map))
+        sent[...] = rows_first([pack_pair(first), last])
+
+    @pl.when(odd)
+    def _():
+        entry = unpack_pair(shared[1, :TILE])
         a, c = load_map(cores.at[0])
-        store(state, sandwich(entry, a, unpack_pair(c)))
-
-    last = sandwich_packed(entry, *load_map(last_map))
-    first = sandwich(load(state), load(transfer), load(green, 0))
-    sent[...] = rows_first([pack_pair(first), last])
+        finish(entry, sandwich(entry, a, unpack_pair(c)))
+
+    @pl.when(jnp.logical_not(odd))
+    def _():
+        entry = unpack_pair(shared[1, :TILE])
+        finish(entry, entry)
 
 
 def split(table):
@@ -297,7 +308,7 @@
         for b in range(2):
             screen[b] = shared[0, b * points : (b + 1) * points]
 
-    g = jnp.swapaxes(values[...].astype(F32), 0, 1)
+    g = jnp.swapaxes(values[...], 0, 1).astype(F32)
     x = [g[0], g[1], screen[0].astype(F32), screen[1].astype(F32)]
     _, col = place_of((points, 2 * TILE))
     left = col < TILE
@@ -336,7 +347,7 @@
 
 
 def unpack_kernel(packed, out, block, left):
-    parts = jnp.swapaxes(packed[...].astype(F32), 0, 1)
+    parts = jnp.swapaxes(packed[...], 0, 1)
     copies = []
     for b in range(2):
         store(block, unpack_pair(parts[b]), b)
@@ -386,8 +397,6 @@
         return lax.all_gather(x, "space", axis_index_groups=groups)
 
     both = [[2 * c, 2 * c + 1] for c in range(8)]
-    outer = chip_groups([(0, 2), (1, 3), (4, 6), (5, 7)])
-    inner = chip_groups([(0, 1), (2, 4), (3, 5), (6, 7)])
     packed = shape(TILE, 2 * PACKED)
     points = TILE
     leaving = [shape(2 * points, 2 * PACKED), shape(2, points, 2 * PACKED)]
@@ -395,22 +404,18 @@
     def chain(cores):
         chip = call(compose_kernel, shape(MAP, 2 * TILE), [VM], interpret=interpret)(cores)
         chips = gather(chip, chip_groups([(0, 1), (2, 3), (4, 5), (6, 7)]))
-        pair_a, end, prefix = call(
-            pair_kernel, [shape(2, n, n), packed, packed], [VM], interpret=interpret
-        )(chips)
-        pair_c = end
-        for hop in (1, 2):
-            received = gather(end, outer if hop % 2 else inner)
-            end, prefix = call(
-                lambda *refs, hop=hop: hop_kernel(hop, *refs),
-                [packed] * 2,
-                [VM] * 5,
-                interpret=interpret,
-            )(received, pair_a, pair_c, end, prefix)
-        received = gather(end, outer)
-        leave, unused = call(
-            lambda *refs: entry_kernel(3, *refs), leaving, [VM] * 3, interpret=interpret
-        )(received, prefix, chips)
+        pair = call(compose_kernel, shape(MAP, 2 * TILE), [VM], interpret=interpret)(chips)
+        pairs = gather(pair, chip_groups([(0, 2), (1, 3), (4, 6), (5, 7)]))
+        end, before, onward = call(
+            middle_kernel,
+            [packed, packed, shape(MAP, 2 * TILE)],
+            [VM] * 2,
+            interpret=interpret,
+        )(pairs, chips)
+        received = gather(end, chip_groups([(0, 7), (1, 6), (2, 5), (3, 4)]))
+        leave, unused = call(entry_kernel, leaving, [VM] * 3, interpret=interpret)(
+            received, before, onward
+        )
         return leave, unused, chip
 
     def exchange_screen(cores):
@@ -431,7 +436,6 @@
         final_kernel,
         shape(TILE, 2, 2 * PACKED),
         [VM] * 5,
-        scratch=[pltpu.VMEM((2, n, n), BF16)],
         interpret=interpret,
     )(shared, cores, last_map, transfer, green)
     return sent, shared, mine

time: 92 us -> 90.1 us (0.979); the launches traced: 90.5 us -> 89.5 us
  no operation moved by 1% of the time
where the time goes in v6:
time: 90.1 us; the launch traced here: 89.5 us
  blocking collectives  83.1 us (92%)
  Pallas kernels  6.34 us (7%)
    all_to_all x3, blocking collectives, exchange(): return lax.all_to_all(x, 'energy', split_axis=0, concat_axis=0, tiled=True)  78.5 us
    all_gather x2, blocking collectives, gather(): return lax.all_gather(x, 'space', axis_index_groups=groups)  4.54 us
    pallas_call x1, Pallas kernels, scan_blocks(): call(local_kernel, [shape(2, n, n), shape(MAP + 2 * PACKED, 2 * TILE)], [...  2.61 us

profile of v6, /device:TPU:14, one launch (start us, length us, event | category | flops | bytes accessed | tf_op | source)
XLA Modules:
  0.0 89.5 jit_solution(16703964115523395598)
XLA Ops:
  0.0 2.6 %shard_map.55 = (bf16[2,192,192]{2,1,0:T(8,128)(2,1)S(1)}, bf16[1536,128]{1,0:T(8,128)(2,1)S(1)}) custom-call(bf16[2,2,192,192]{3,2,1,0:T(8,128)(2,1)} %bitcast.13, bf16[2,192,192]{2,1,0:T(8,128)(2,1)} %coupling.1, bf16[2,2,192,192]{3,2,1,0:T(8,128)(2,1)} %bitcast.19), custom_call_target="tpu_custom_call" | custom-call | tf_op jit(solution)/shard_map/pallas_call | solution.py:383
  2.6 2.4 %all-gather.3 = bf16[3072,128]{1,0:T(8,128)(2,1)S(1)} all-gather(bf16[1536,128]{1,0:T(8,128)(2,1)S(1)} %get-tuple-element.21), channel_id=5, replica_groups={{0,1},{2,3},{4,5},{6,7},{8,9},{10,11},{12,13},{14,15},{16,17},{18,19},{..., dimensions={0}, use_global_device_ids=true | all-gather | bytes 1179648 | tf_op jit(solution)/shard_map/all_gather | solution.py:397
  5.0 37.5 %conditional.1 = (bf16[128,640]{1,0:T(8,128)(2,1)S(1)}, bf16[2,64,640]{2,1,0:T(8,128)(2,1)S(1)}, bf16[896,128]{1,0:T(8,128)(2,1)S(1)}) conditional(s32[]{:T(128)} %convert_element_type.3, bf16[2,1536,128]{2,1,0:T(8,128)(2,1)S(1)} %bitcast.16, bf16[2,1536,128]{2,1,0:T(8,128)(2,1)S(1)} %bitcast.17), branch_computations={%region_0.1_spmd, %region_1.2_spmd} | conditional | bytes 3457104 | solution.py:433
  5.0 0.2 branch_0_fun.2
  5.2 37.2 %all_to_all.14.values = bf16[64,4,640]{2,1,0:T(4,128)(2,1)S(1)} all-to-all(bf16[64,4,640]{2,1,0:T(4,128)(2,1)S(1)} %get-tuple-element.7), channel_id=1, replica_groups=mesh['energy'=64,'space'=16] {'energy'}, dimensions={0} | all-to-all | bytes 655360 | tf_op jit(solution)/shard_map/cond/branch_0_fun/all_to_all | solution.py:449
  42.4 0.1 branch_0_fun.3
  42.5 0.0 copy-start
  42.5 2.2 %all-gather.4 = bf16[256,640]{1,0:T(8,128)(2,1)S(1)} all-gather(bf16[128,640]{1,0:T(8,128)(2,1)S(1)} %get-tuple-element.22), channel_id=6, replica_groups={{0,1},{2,3},{4,5},{6,7},{8,9},{10,11},{12,13},{14,15},{16,17},{18,19},{..., dimensions={0}, use_global_device_ids=true | all-gather | bytes 491520 | tf_op jit(solution)/shard_map/all_gather | solution.py:397
  44.7 0.0 copy-done
  44.7 1.5 %shard_map.56 = bf16[64,2,640]{2,1,0:T(2,128)(2,1)S(1)} custom-call(bf16[2,128,640]{2,1,0:T(8,128)(2,1)S(1)} %bitcast.10, bf16[2,1536,128]{2,1,0:T(8,128)(2,1)S(1)} %bitcast.18, bf16[896,128]{1,0:T(8,128)(2,1)S(1)} %get-tuple-element.23.last_map, bf16[2,192,192]{2,1,0:T(8,128)(2,1)S(1)} %get-tuple-element.24.transfer, bf16[2,2,192,192]{3,2,1,0:T(8,128)(2,1)S(1)} %bitcast.14), custom_call_target="tpu_custom_call" | custom-call | tf_op jit(solution)/shard_map/pallas_call | solution.py:435
  46.2 0.0 copy-start.1
  46.2 0.0 copy-start.2
  46.2 24.5 %all_to_all.15.values = bf16[64,2,640]{2,1,0:T(2,128)(2,1)S(1)} all-to-all(bf16[64,2,640]{2,1,0:T(2,128)(2,1)S(1)} %shard_map.56), channel_id=1, replica_groups=mesh['energy'=64,'space'=16] {'energy'}, dimensions={0} | all-to-all | bytes 327680 | tf_op jit(solution)/shard_map/all_to_all | solution.py:449
  70.7 0.0 copy-done.1
  70.7 0.0 copy-done.2
  70.7 0.8 shard_map.57
  71.5 16.8 %all_to_all.16.packed = bf16[64,2,640]{2,1,0:T(2,128)(2,1)S(1)} all-to-all(bf16[64,2,640]{2,1,0:T(2,128)(2,1)S(1)} %shard_map.57), channel_id=1, replica_groups=mesh['energy'=64,'space'=16] {'energy'}, dimensions={0} | all-to-all | bytes 327680 | tf_op jit(solution)/shard_map/all_to_all | solution.py:449
  88.2 1.3 %shard_map.58 = bf16[2,2,192,192]{3,2,1,0:T(8,128)(2,1)} custom-call(bf16[64,2,640]{2,1,0:T(2,128)(2,1)S(1)} %all_to_all.16.packed), custom_call_target="tpu_custom_call" | custom-call | tf_op jit(solution)/shard_map/pallas_call | solution.py:459
Async XLA Ops:
  42.5 2.2 %copy-start = (bf16[1,2,2,192,192]{4,3,2,1,0:T(8,128)(2,1)S(1)}, bf16[1,2,2,192,192]{4,3,2,1,0:T(8,128)(2,1)}, u32[]{:S(2)}) copy-start(bf16[1,2,2,192,192]{4,3,2,1,0:T(8,128)(2,1)} %param.7) | copy-start | bytes 884740
  46.2 24.5 %copy-start.1 = (bf16[128,256]{1,0:T(8,128)(2,1)S(1)}, bf16[128,256]{1,0:T(8,128)(2,1)}, u32[]{:S(2)}) copy-start(bf16[128,256]{1,0:T(8,128)(2,1)} %constant.23.clone.inverse) | copy-start | bytes 196612
  46.2 24.5 %copy-start.2 = (bf16[128,256]{1,0:T(8,128)(2,1)S(1)}, bf16[128,256]{1,0:T(8,128)(2,1)}, u32[]{:S(2)}) copy-start(bf16[128,256]{1,0:T(8,128)(2,1)} %constant.22.clone.forward) | copy-start | bytes 196612

commit v7 on v6

--- a/solution.py
+++ b/solution.py
@@ -70,9 +70,8 @@
     top, mid = m[:t, : 2 * t], m[t : 2 * t, : 2 * t]
     right = [widened(m[k * t : (k + 1) * t, 2 * t :]) for k in range(3)]
     left = col < t
-    d1 = jnp.where(col == row + t, mid, 0.0)
-    diagonal = jnp.sum(d1, axis=1, keepdims=True)
-    spare = jnp.where(col == 0, diagonal, jnp.where((row == 2) & (col == 1), diagonal[:1], 0.0))
+    corner = (row == 2) & (col == 0)
+    spare = jnp.where(corner, mid[:1, t : t + 1], jnp.where(col == row - 1, pltpu.roll(mid, t - 1, 1), 0.0))
     shared = jnp.where(col - t >= row, half_turn(top), mid)
     last = jnp.where(col >= row, right[2], spare)
     return jnp.where(left, right[0], top), jnp.where(left, right[1], shared), last
@@ -84,7 +83,7 @@
     left = col < t
     first_t, second_t = first.T, second.T
     t02, t01, t12, x_t = first_t[:t], first_t[t:], second_t[:t], second_t[t:]
-    diagonal = jnp.where(row[:, :1] == 0, y[2:3, 1:2], y[:, :1])
+    diagonal = jnp.where(row == 0, y[2:3, :1], pltpu.roll(y, t + 1, 1))
     d0 = jnp.where(col >= row, half_turn(second), widened(x_t))
     d1 = jnp.where(
         col - t < row, second, jnp.where(col - t > row, widened(x_t), diagonal)
@@ -210,10 +209,6 @@
     def _():
         end[...] = first
 
-    @pl.when(pair < 3)
-    def _():
-        onward[...] = chips[0]
-
     @pl.when((pair == 3) & jnp.logical_not(odd))
     def _():
         onward[...] = pairs[0]
@@ -227,19 +222,20 @@
     return jnp.swapaxes(jnp.stack([p.astype(BF16) for p in parts], axis=0), 0, 1)
 
 
-def entry_kernel(received, before_in, onward, entry, unused):
+def entry_kernel(received, before_in, chips, onward, entry, unread):
     index = lax.axis_index("space")
     pair, odd = index // 4, index // 2 % 2 == 1
     before = jnp.where(pair < 2, before_in[...], received[0])
-    unused[...] = jnp.zeros(unused.shape, BF16)
-    entry[TILE:] = jnp.zeros((TILE, 2 * PACKED), BF16)
-    moved = odd | (pair == 3)
-
-    @pl.when(moved)
+
+    @pl.when(pair == 3)
     def _():
         entry[:TILE] = sandwich_packed(unpack_pair(before), *load_map(onward))
 
-    @pl.when(jnp.logical_not(moved))
+    @pl.when((pair < 3) & odd)
+    def _():
+        entry[:TILE] = sandwich_packed(unpack_pair(before), *load_map(chips.at[0]))
+
+    @pl.when((pair < 3) & jnp.logical_not(odd))
     def _():
         entry[:TILE] = before
 
@@ -350,9 +346,11 @@
     parts = jnp.swapaxes(packed[...], 0, 1)
     copies = []
     for b in range(2):
-        store(block, unpack_pair(parts[b]), b)
-        copies.append(pltpu.make_async_copy(block.at[b], out.at[b], left.at[b]))
-        copies[b].start()
+        for part, matrix in enumerate(unpack_pair(parts[b])):
+            block[b, part] = matrix
+            copy = pltpu.make_async_copy(block.at[b, part], out.at[b, part], left.at[b, part])
+            copy.start()
+            copies.append(copy)
     for copy in copies:
         copy.wait()
 
@@ -413,8 +411,8 @@
             interpret=interpret,
         )(pairs, chips)
         received = gather(end, chip_groups([(0, 7), (1, 6), (2, 5), (3, 4)]))
-        leave, unused = call(entry_kernel, leaving, [VM] * 3, interpret=interpret)(
-            received, before, onward
+        leave, unused = call(entry_kernel, leaving, [VM] * 4, interpret=interpret)(
+            received, before, chips, onward
         )
         return leave, unused, chip
 
@@ -460,7 +458,7 @@
         unpack_kernel,
         shape(2, 2, n, n),
         [VM],
-        scratch=[pltpu.VMEM((2, 2, n, n), BF16), pltpu.SemaphoreType.DMA((2,))],
+        scratch=[pltpu.VMEM((2, 2, n, n), BF16), pltpu.SemaphoreType.DMA((2, 2))],
         out_spec=HB,
     )(exchange(result))[None]
 

time: 90.1 us -> 89.2 us (0.990)
  no operation moved by 1% of the time
where the time goes in v7:
time: 89.2 us; the launch traced here: 88.8 us
  blocking collectives  82.6 us (93%)
  Pallas kernels  6.12 us (7%)
    all_to_all x3, blocking collectives, exchange(): return lax.all_to_all(x, 'energy', split_axis=0, concat_axis=0, tiled=True)  78.1 us
    all_gather x2, blocking collectives, gather(): return lax.all_gather(x, 'space', axis_index_groups=groups)  4.54 us
    pallas_call x1, Pallas kernels, scan_blocks(): call(local_kernel, [shape(2, n, n), shape(MAP + 2 * PACKED, 2 * TILE)], [...  2.53 us

profile of v7, /device:TPU:14, one launch (start us, length us, event | category | flops | bytes accessed | tf_op | source)
XLA Modules:
  0.0 88.8 jit_solution(9080474834959832599)
XLA Ops:
  0.0 2.5 %shard_map.55 = (bf16[2,192,192]{2,1,0:T(8,128)(2,1)S(1)}, bf16[1536,128]{1,0:T(8,128)(2,1)S(1)}) custom-call(bf16[2,2,192,192]{3,2,1,0:T(8,128)(2,1)} %bitcast.14, bf16[2,192,192]{2,1,0:T(8,128)(2,1)} %coupling.1, bf16[2,2,192,192]{3,2,1,0:T(8,128)(2,1)} %bitcast.20), custom_call_target="tpu_custom_call" | custom-call | tf_op jit(solution)/shard_map/pallas_call | solution.py:381
  2.5 2.4 %all-gather.3 = bf16[3072,128]{1,0:T(8,128)(2,1)S(1)} all-gather(bf16[1536,128]{1,0:T(8,128)(2,1)S(1)} %get-tuple-element.21), channel_id=5, replica_groups={{0,1},{2,3},{4,5},{6,7},{8,9},{10,11},{12,13},{14,15},{16,17},{18,19},{..., dimensions={0}, use_global_device_ids=true | all-gather | bytes 1179648 | tf_op jit(solution)/shard_map/all_gather | solution.py:395
  4.9 37.5 %conditional.1 = (bf16[128,640]{1,0:T(8,128)(2,1)S(1)}, bf16[2,64,640]{2,1,0:T(8,128)(2,1)S(1)}, bf16[896,128]{1,0:T(8,128)(2,1)S(1)}) conditional(s32[]{:T(128)} %convert_element_type.3, bf16[2,1536,128]{2,1,0:T(8,128)(2,1)S(1)} %bitcast.17, bf16[2,1536,128]{2,1,0:T(8,128)(2,1)S(1)} %bitcast.18), branch_computations={%region_0.1_spmd, %region_1.2_spmd} | conditional | bytes 3457104 | solution.py:431
  4.9 0.2 branch_0_fun.2
  5.1 37.2 %all_to_all.14.values = bf16[64,4,640]{2,1,0:T(4,128)(2,1)S(1)} all-to-all(bf16[64,4,640]{2,1,0:T(4,128)(2,1)S(1)} %get-tuple-element.7), channel_id=1, replica_groups=mesh['energy'=64,'space'=16] {'energy'}, dimensions={0} | all-to-all | bytes 655360 | tf_op jit(solution)/shard_map/cond/branch_0_fun/all_to_all | solution.py:447
  42.3 0.1 branch_0_fun.3
  42.4 0.0 copy-start
  42.4 2.2 %all-gather.4 = bf16[256,640]{1,0:T(8,128)(2,1)S(1)} all-gather(bf16[128,640]{1,0:T(8,128)(2,1)S(1)} %get-tuple-element.22), channel_id=6, replica_groups={{0,1},{2,3},{4,5},{6,7},{8,9},{10,11},{12,13},{14,15},{16,17},{18,19},{..., dimensions={0}, use_global_device_ids=true | all-gather | bytes 491520 | tf_op jit(solution)/shard_map/all_gather | solution.py:395
  44.6 0.0 copy-done
  44.6 1.3 %shard_map.56 = bf16[64,2,640]{2,1,0:T(2,128)(2,1)S(1)} custom-call(bf16[2,128,640]{2,1,0:T(8,128)(2,1)S(1)} %bitcast.11, bf16[2,1536,128]{2,1,0:T(8,128)(2,1)S(1)} %bitcast.19, bf16[896,128]{1,0:T(8,128)(2,1)S(1)} %get-tuple-element.23.last_map, bf16[2,192,192]{2,1,0:T(8,128)(2,1)S(1)} %get-tuple-element.24.transfer, bf16[2,2,192,192]{3,2,1,0:T(8,128)(2,1)S(1)} %bitcast.15), custom_call_target="tpu_custom_call" | custom-call | tf_op jit(solution)/shard_map/pallas_call | solution.py:433
  45.9 0.0 copy-start.1
  45.9 0.0 copy-start.2
  46.0 24.1 %all_to_all.15.values = bf16[64,2,640]{2,1,0:T(2,128)(2,1)S(1)} all-to-all(bf16[64,2,640]{2,1,0:T(2,128)(2,1)S(1)} %shard_map.56), channel_id=1, replica_groups=mesh['energy'=64,'space'=16] {'energy'}, dimensions={0} | all-to-all | bytes 327680 | tf_op jit(solution)/shard_map/all_to_all | solution.py:447
  70.0 0.0 copy-done.1
  70.0 0.0 copy-done.2
  70.0 0.8 shard_map.57
  70.8 16.8 %all_to_all.16.packed = bf16[64,2,640]{2,1,0:T(2,128)(2,1)S(1)} all-to-all(bf16[64,2,640]{2,1,0:T(2,128)(2,1)S(1)} %shard_map.57), channel_id=1, replica_groups=mesh['energy'=64,'space'=16] {'energy'}, dimensions={0} | all-to-all | bytes 327680 | tf_op jit(solution)/shard_map/all_to_all | solution.py:447
  87.6 1.3 %shard_map.58 = bf16[2,2,192,192]{3,2,1,0:T(8,128)(2,1)} custom-call(bf16[64,2,640]{2,1,0:T(2,128)(2,1)S(1)} %all_to_all.16.packed), custom_call_target="tpu_custom_call" | custom-call | tf_op jit(solution)/shard_map/pallas_call | solution.py:457
Async XLA Ops:
  42.4 2.2 %copy-start = (bf16[1,2,2,192,192]{4,3,2,1,0:T(8,128)(2,1)S(1)}, bf16[1,2,2,192,192]{4,3,2,1,0:T(8,128)(2,1)}, u32[]{:S(2)}) copy-start(bf16[1,2,2,192,192]{4,3,2,1,0:T(8,128)(2,1)} %param.7) | copy-start | bytes 884740
  45.9 24.1 %copy-start.1 = (bf16[128,256]{1,0:T(8,128)(2,1)S(1)}, bf16[128,256]{1,0:T(8,128)(2,1)}, u32[]{:S(2)}) copy-start(bf16[128,256]{1,0:T(8,128)(2,1)} %constant.23.clone.inverse) | copy-start | bytes 196612
  45.9 24.1 %copy-start.2 = (bf16[128,256]{1,0:T(8,128)(2,1)S(1)}, bf16[128,256]{1,0:T(8,128)(2,1)}, u32[]{:S(2)}) copy-start(bf16[128,256]{1,0:T(8,128)(2,1)} %constant.22.clone.forward) | copy-start | bytes 196612

commit v8 on v7

--- a/solution.py
+++ b/solution.py
@@ -151,8 +151,9 @@
 
 
 def local_kernel(
-    green, coupling, screened, transfer, aggregate, green_in, coupling_in, screened_in, arrived
+    green, coupling, screened, transfer, own, sent, green_in, coupling_in, screened_in, arrived
 ):
+    odd = lax.axis_index("space") % 2 == 1
     copies = [
         [
             pltpu.make_async_copy(coupling.at[b], coupling_in.at[b], arrived.at[b, 0]),
@@ -165,8 +166,14 @@
         pltpu.make_async_copy(screened.at[b], screened_in.at[b], arrived.at[b, 3])
         for b in range(2)
     ]
-    for copy in copies[0] + copies[1] + later:
+    for copy in copies[0] + copies[1]:
         copy.start()
+
+    @pl.when(odd)
+    def _():
+        for copy in later:
+            copy.start()
+
     maps = []
     for b in range(2):
         for copy in copies[b]:
@@ -179,10 +186,17 @@
         maps.append((t, g))
     (t0, g0), (t1, g1) = maps
     c = pack_pair(sandwich(g0, t1, g1)).astype(BF16)
-    store_map(aggregate, rounded(complex_product(t1, t0, dot_nn)), c)
-    for b in range(2):
-        later[b].wait()
-        store_slabs(aggregate, MAP + b * PACKED, pack_pair(load(screened_in, b)).astype(BF16))
+    store_map(own, rounded(complex_product(t1, t0, dot_nn)), c)
+
+    @pl.when(odd)
+    def _():
+        for b in range(2):
+            later[b].wait()
+            store_slabs(sent, b * PACKED, pack_pair(load(screened_in, b)).astype(BF16))
+
+    @pl.when(jnp.logical_not(odd))
+    def _():
+        sent[...] = own[...]
 
 
 def joined(low, high):
@@ -193,6 +207,10 @@
 
 def compose_kernel(maps, out):
     store_map(out, *joined(maps.at[0], maps.at[1]))
+
+
+def chip_kernel(cores, own, out):
+    store_map(out, *joined(cores.at[0], own))
 
 
 def middle_kernel(pairs, chips, end, before, onward):
@@ -240,11 +258,10 @@
         entry[:TILE] = before
 
 
-def screen_kernel(cores, sent, last_map):
-    last_map[...] = cores[0, :MAP]
-    sent[...] = rows_first(
-        [load_slabs(cores.at[core], MAP + b * PACKED) for core in range(2) for b in range(2)]
-    )
+def screen_kernel(cores, own, screened, sent, last_map):
+    last_map[...] = own[...]
+    mine = [pack_pair(load(screened, b)).astype(BF16) for b in range(2)]
+    sent[...] = rows_first(mine + [load_slabs(cores.at[1], b * PACKED) for b in range(2)])
 
 
 def regroup_kernel(values, theirs, mine):
@@ -378,9 +395,9 @@
 
 def scan_blocks(green, coupling, screened, exchange, interpret=False):
     n = green.shape[-1]
-    transfer, aggregate = call(
+    transfer, own, aggregate = call(
         local_kernel,
-        [shape(2, n, n), shape(MAP + 2 * PACKED, 2 * TILE)],
+        [shape(2, n, n), shape(MAP, 2 * TILE), shape(MAP, 2 * TILE)],
         [HB] * 3,
         scratch=[
             pltpu.VMEM((2, 2, n, n), BF16),
@@ -399,8 +416,8 @@
     points = TILE
     leaving = [shape(2 * points, 2 * PACKED), shape(2, points, 2 * PACKED)]
 
-    def chain(cores):
-        chip = call(compose_kernel, shape(MAP, 2 * TILE), [VM], interpret=interpret)(cores)
+    def chain(cores, own, screened):
+        chip = call(chip_kernel, shape(MAP, 2 * TILE), [VM] * 2, interpret=interpret)(cores, own)
         chips = gather(chip, chip_groups([(0, 1), (2, 3), (4, 5), (6, 7)]))
         pair = call(compose_kernel, shape(MAP, 2 * TILE), [VM], interpret=interpret)(chips)
         pairs = gather(pair, chip_groups([(0, 2), (1, 3), (4, 6), (5, 7)]))
@@ -416,19 +433,19 @@
         )
         return leave, unused, chip
 
-    def exchange_screen(cores):
+    def exchange_screen(cores, own, screened):
         sent, last_map = call(
             screen_kernel,
             [shape(TILE, 4, 2 * PACKED), shape(MAP, 2 * TILE)],
-            [VM],
+            [VM] * 3,
             interpret=interpret,
-        )(cores)
+        )(cores, own, screened)
         leave, mine = call(regroup_kernel, leaving, [VM], interpret=interpret)(exchange(sent))
         return leave, mine, last_map
 
     cores = gather(aggregate, both)
     odd = lax.axis_index("space") % 2 == 1
-    leave, mine, last_map = lax.cond(odd, chain, exchange_screen, cores)
+    leave, mine, last_map = lax.cond(odd, chain, exchange_screen, cores, own, screened)
     shared = gather(leave, both)
     sent = call(
         final_kernel,

time: 89.2 us -> 88.8 us (level)
  no operation moved by 1% of the time
where the time goes in v8:
time: 88.8 us; the launch traced here: 88.4 us
  blocking collectives  82.3 us (93%)
  Pallas kernels  5.95 us (7%)
    all_to_all x3, blocking collectives, exchange(): return lax.all_to_all(x, 'energy', split_axis=0, concat_axis=0, tiled=True)  77.9 us
    all_gather x2, blocking collectives, gather(): return lax.all_gather(x, 'space', axis_index_groups=groups)  4.44 us
    pallas_call x1, Pallas kernels, scan_blocks(): call(local_kernel, [shape(2, n, n), shape(MAP, 2 * TILE), shape(MAP, 2 *...  2.18 us

profile of v8, /device:TPU:14, one launch (start us, length us, event | category | flops | bytes accessed | tf_op | source)
XLA Modules:
  0.0 88.4 jit_solution(6918972580405066059)
XLA Ops:
  0.0 2.2 %shard_map.55 = (bf16[2,192,192]{2,1,0:T(8,128)(2,1)S(1)}, bf16[896,128]{1,0:T(8,128)(2,1)S(1)}, bf16[896,128]{1,0:T(8,128)(2,1)S(1)}) custom-call(bf16[2,2,192,192]{3,2,1,0:T(8,128)(2,1)} %bitcast.14, bf16[2,192,192]{2,1,0:T(8,128)(2,1)} %coupling.1, bf16[2,2,192,192]{3,2,1,0:T(8,128)(2,1)} %bitcast.20), custom_call_target="tpu_custom_call" | custom-call | tf_op jit(solution)/shard_map/pallas_call | solution.py:398
  2.2 0.0 copy-start.3
  2.2 2.3 %all-gather.3 = bf16[1792,128]{1,0:T(8,128)(2,1)S(1)} all-gather(bf16[896,128]{1,0:T(8,128)(2,1)S(1)} %get-tuple-element.35), channel_id=5, replica_groups={{0,1},{2,3},{4,5},{6,7},{8,9},{10,11},{12,13},{14,15},{16,17},{18,19},{..., dimensions={0}, use_global_device_ids=true | all-gather | bytes 688128 | tf_op jit(solution)/shard_map/all_gather | solution.py:412
  4.5 0.0 copy-done.3
  4.5 37.7 %conditional.1 = (bf16[128,640]{1,0:T(8,128)(2,1)S(1)}, bf16[2,64,640]{2,1,0:T(8,128)(2,1)S(1)}, bf16[896,128]{1,0:T(8,128)(2,1)S(1)}) conditional(s32[]{:T(128)} %convert_element_type.3, (bf16[2,896,128]{2,1,0:T(8,128)(2,1)S(1)}, bf16[896,128]{1,0:T(8,128)(2,1)S(1)}, bf16[2,2,192,192]{3,2,1,0:T(8,128)(2,1)S(1)}) %tuple.19, ...), branch_computations={%region_0.1_spmd, %region_1.2_spmd} | conditional | bytes 3457104 | solution.py:448
  4.5 0.4 branch_0_fun.2
  4.8 37.2 %all_to_all.14.values = bf16[64,4,640]{2,1,0:T(4,128)(2,1)S(1)} all-to-all(bf16[64,4,640]{2,1,0:T(4,128)(2,1)S(1)} %get-tuple-element.18), channel_id=1, replica_groups=mesh['energy'=64,'space'=16] {'energy'}, dimensions={0} | all-to-all | bytes 655360 | tf_op jit(solution)/shard_map/cond/branch_0_fun/all_to_all | solution.py:464
  42.1 0.1 branch_0_fun.3
  42.2 0.0 copy-start
  42.2 2.2 %all-gather.4 = bf16[256,640]{1,0:T(8,128)(2,1)S(1)} all-gather(bf16[128,640]{1,0:T(8,128)(2,1)S(1)} %get-tuple-element.37), channel_id=6, replica_groups={{0,1},{2,3},{4,5},{6,7},{8,9},{10,11},{12,13},{14,15},{16,17},{18,19},{..., dimensions={0}, use_global_device_ids=true | all-gather | bytes 491520 | tf_op jit(solution)/shard_map/all_gather | solution.py:412
  44.4 0.0 copy-done
  44.4 1.3 %shard_map.56 = bf16[64,2,640]{2,1,0:T(2,128)(2,1)S(1)} custom-call(bf16[2,128,640]{2,1,0:T(8,128)(2,1)S(1)} %bitcast.11, bf16[2,896,128]{2,1,0:T(8,128)(2,1)S(1)} %bitcast.19, bf16[896,128]{1,0:T(8,128)(2,1)S(1)} %get-tuple-element.38.last_map, bf16[2,192,192]{2,1,0:T(8,128)(2,1)S(1)} %get-tuple-element.39.transfer, bf16[2,2,192,192]{3,2,1,0:T(8,128)(2,1)S(1)} %bitcast.15), custom_call_target="tpu_custom_call" | custom-call | tf_op jit(solution)/shard_map/pallas_call | solution.py:450
  45.7 0.0 copy-start.1
  45.7 0.0 copy-start.2
  45.7 23.9 %all_to_all.15.values = bf16[64,2,640]{2,1,0:T(2,128)(2,1)S(1)} all-to-all(bf16[64,2,640]{2,1,0:T(2,128)(2,1)S(1)} %shard_map.56), channel_id=1, replica_groups=mesh['energy'=64,'space'=16] {'energy'}, dimensions={0} | all-to-all | bytes 327680 | tf_op jit(solution)/shard_map/all_to_all | solution.py:464
  69.6 0.0 copy-done.1
  69.6 0.0 copy-done.2
  69.6 0.8 shard_map.57
  70.4 16.7 %all_to_all.16.packed = bf16[64,2,640]{2,1,0:T(2,128)(2,1)S(1)} all-to-all(bf16[64,2,640]{2,1,0:T(2,128)(2,1)S(1)} %shard_map.57), channel_id=1, replica_groups=mesh['energy'=64,'space'=16] {'energy'}, dimensions={0} | all-to-all | bytes 327680 | tf_op jit(solution)/shard_map/all_to_all | solution.py:464
  87.1 1.3 %shard_map.58 = bf16[2,2,192,192]{3,2,1,0:T(8,128)(2,1)} custom-call(bf16[64,2,640]{2,1,0:T(2,128)(2,1)S(1)} %all_to_all.16.packed), custom_call_target="tpu_custom_call" | custom-call | tf_op jit(solution)/shard_map/pallas_call | solution.py:474
Async XLA Ops:
  2.2 2.3 %copy-start.3 = (bf16[1,2,2,192,192]{4,3,2,1,0:T(8,128)(2,1)S(1)}, bf16[1,2,2,192,192]{4,3,2,1,0:T(8,128)(2,1)}, u32[]{:S(2)}) copy-start(bf16[1,2,2,192,192]{4,3,2,1,0:T(8,128)(2,1)} %param.9) | copy-start | bytes 884740
  42.2 2.2 %copy-start = (bf16[1,2,2,192,192]{4,3,2,1,0:T(8,128)(2,1)S(1)}, bf16[1,2,2,192,192]{4,3,2,1,0:T(8,128)(2,1)}, u32[]{:S(2)}) copy-start(bf16[1,2,2,192,192]{4,3,2,1,0:T(8,128)(2,1)} %param.7) | copy-start | bytes 884740
  45.7 23.9 %copy-start.1 = (bf16[128,256]{1,0:T(8,128)(2,1)S(1)}, bf16[128,256]{1,0:T(8,128)(2,1)}, u32[]{:S(2)}) copy-start(bf16[128,256]{1,0:T(8,128)(2,1)} %constant.23.clone.inverse) | copy-start | bytes 196612
  45.7 23.9 %copy-start.2 = (bf16[128,256]{1,0:T(8,128)(2,1)S(1)}, bf16[128,256]{1,0:T(8,128)(2,1)}, u32[]{:S(2)}) copy-start(bf16[128,256]{1,0:T(8,128)(2,1)} %constant.22.clone.forward) | copy-start | bytes 196612
